TPU v7x, 32 devices: a whole 2x2x4 slice. The times are simulated.
32 devices in a mesh: doc: 2 (over core), coarse: 2 (over x), fine: 8 (over z, y).
Axes of the slice: x: 2, y: 2, z: 4, core: 2. Of those that a mesh axis runs over, the one named last changes fastest.
Arguments:
- q_light: bfloat16 [2, 2048, 1024], P('doc', ('coarse', 'fine')), may hold values from -8 to 8
- k_light: bfloat16 [2, 2048, 1024], P('doc', ('coarse', 'fine')), may hold values from -8 to 8
- v_light: bfloat16 [2, 2048, 1024], P('doc', ('coarse', 'fine')), may hold values from -6 to 6
- q_heavy: bfloat16 [2, 2048, 1024], P('doc', ('coarse', 'fine')), may hold values from -8 to 8
- k_heavy: bfloat16 [2, 2048, 1024], P('doc', ('coarse', 'fine')), may hold values from -8 to 8
- v_heavy: bfloat16 [2, 2048, 1024], P('doc', ('coarse', 'fine')), may hold values from -6 to 6
- enc_kv: bfloat16 [2, 2048, 128], P('doc', ('coarse', 'fine')), may hold values from -8 to 8
- dec_queries: bfloat16 [2, 512, 1024], P('doc'), may hold values from -8 to 8
- query_ids: int32 [2, 16], P('doc'), may hold values from 0 to 15, as said below
- key_ids: int32 [2, 16], P('doc'), may hold values from 0 to 15, as said below
Outputs:
- encoded: bfloat16 [2, 2048, 1024], P('doc', ('coarse', 'fine'))
- decoded: bfloat16 [2, 512, 1024], P('doc')
Inputs may be any that keep to these rules, and one draw needn't show every extreme that they name: `query_ids`: for each document and each c below the number of coarse groups, entries c * 8 to (c + 1) * 8 - 1 are distinct block numbers among blocks c * 8 to (c + 1) * 8 - 1 (so every block of the group is listed), and entry c * 8 + f is the block assigned to the f-th device of that group. `key_ids`: for each document and each c below the number of coarse groups, entries c * 8 to (c + 1) * 8 - 1 are distinct block numbers among blocks c * 8 * 1 to (c + 1) * 8 - 1.
All inputs are finite; a program needn't handle non-finite values.
Results may differ from a plain program's by a relative error of at most 0.009.
Values may be sent and summed in bfloat16 or wider, within the bound.
A program may use at most 384 MiB of HBM per device.

v0:
```python
import functools

import jax
import jax.numpy as jnp
from jax import lax
from jax.experimental import pallas as pl
from jax.experimental.pallas import tpu as pltpu
from jax.sharding import PartitionSpec as P

HEAD = 64
PAIR = 2 * HEAD
ROUTED_BLOCK = 128
KGRP = 8
LOW = 2
MESH = pl.DeviceIdType.MESH
NEG = -1e30


def dot_t(a, b):
    return lax.dot_general(a, b, (((1,), (1,)), ((), ())), preferred_element_type=jnp.float32)


def dot(a, b):
    return jnp.dot(a, b, preferred_element_type=jnp.float32)


def stacked_pair(q, low_half):
    q = q * jnp.asarray(HEAD ** (-0.5), q.dtype)
    zero = jnp.zeros_like(q)
    return jnp.concatenate([jnp.where(low_half, q, zero), jnp.where(low_half, zero, q)], axis=0)


def kernel(dims, has_bias, *refs):
    n_coarse, n_fine, tokens, width, dec_rows = dims
    n_seq = n_coarse * n_fine
    n_q = n_fine // LOW
    n_kv = n_coarse * LOW
    heads = width // HEAD
    pairs = heads // 2
    refs = list(refs)
    ql, kl, vl, qh, kh, vh, enc, decq = refs[:8]
    bias_ref = refs[8] if has_bias else None
    (out, dec, encbuf, dq, do, qbuf, kbuf, vbuf, khalo, vhalo, osend, orecv, ssend, srecv,
     wts, light, band, enc_s, enc_r, dec_s, dec_r, q_s, q_r, o_s, o_r, st_s, st_r, h_s, h_r,
     ek_s, ek_r, dk_s, dk_r, k_s, k_r, v_s, v_r, drows, load_s) = refs[8 + has_bias:]

    c = lax.axis_index("coarse")
    f = lax.axis_index("fine")
    here = c * n_fine + f
    me_q = lax.div(f, LOW)
    lo = lax.rem(f, LOW)
    me_kv = c * LOW + lo

    def at_seq(s):
        return {"coarse": lax.div(s, n_fine), "fine": lax.rem(s, n_fine)}

    def at_q(a):
        return {"coarse": c, "fine": a * LOW + lo}

    def at_kv(b):
        return {"coarse": lax.div(b, LOW), "fine": me_q * LOW + lax.rem(b, LOW)}

    def remote(src, dst, ssem, rsem, device):
        return pltpu.make_async_remote_copy(
            src_ref=src, dst_ref=dst, send_sem=ssem, recv_sem=rsem,
            device_id=device, device_id_type=MESH,
        )

    def up(me, d, n):
        return lax.rem(me + d, n)

    def down(me, d, n):
        return lax.rem(me + n - d, n)

    load = pltpu.make_async_copy(decq.at[me_kv, me_q], drows, load_s)
    load.start()
    barrier = pltpu.get_barrier_semaphore()

    def greet(d, carry):
        pl.semaphore_signal(barrier, inc=1, device_id=at_seq(up(here, d, n_seq)), device_id_type=MESH)
        return carry

    lax.fori_loop(1, n_seq, greet, 0)
    pl.semaphore_wait(barrier, n_seq - 1)

    def enc_copy(d):
        mine = encbuf.at[me_kv, me_q]
        return remote(enc, mine, enc_s.at[d], enc_r.at[me_q], at_q(up(me_q, d, n_q)))

    def enc_arrival(d):
        src = down(me_q, d, n_q)
        return remote(enc, encbuf.at[me_kv, src], enc_s.at[d], enc_r.at[src], at_q(src))

    def dec_copy(d):
        mine = dec.at[me_kv, me_q]
        return remote(mine, mine, dec_s.at[d], dec_r.at[me_q], at_q(up(me_q, d, n_q)))

    def dec_arrival(d):
        src = down(me_q, d, n_q)
        part = dec.at[me_kv, src]
        return remote(part, part, dec_s.at[d], dec_r.at[src], at_q(src))

    def q_copy(block, way):
        peer = jnp.clip(me_q + way, 0, n_q - 1)
        return remote(qbuf.at[block], qbuf.at[block], q_s.at[block], q_r.at[block], at_q(peer))

    def own_q(way):
        peer = jnp.clip(me_q + way, 0, n_q - 1)
        return remote(qh, qbuf.at[me_q], q_s.at[n_q + int(way > 0)], q_r.at[me_q], at_q(peer))

    def q_step(t):
        for way in (1, -1):
            src = me_q - way * t
            block = jnp.clip(src, 0, n_q - 1)

            @pl.when((src >= 0) & (src < n_q))
            def _():
                q_copy(block, -way).wait_recv()

                @pl.when((me_q + way >= 0) & (me_q + way < n_q))
                def _():
                    q_copy(block, way).start()

    other = c * LOW + 1 - lo

    def plane(src, buf, ss, rs):
        def low():
            return remote(src, buf.at[me_kv], ss.at[0, 0], rs.at[me_kv], at_kv(other))

        def far(d, relay):
            block = other if relay else me_kv
            peer = up(c, d, n_coarse) * LOW + lo
            return remote(buf.at[other] if relay else src, buf.at[block],
                          ss.at[int(relay), d], rs.at[block], at_kv(peer))

        def arrival(block):
            return remote(src, buf.at[block], ss.at[0, 0], rs.at[block], at_kv(block))

        def begin():
            low().start()
            for d in range(1, n_coarse):
                far(d, False).start()

        def relay():
            arrival(other).wait_recv()
            for d in range(1, n_coarse):
                far(d, True).start()

        def arrive():
            for d in range(1, n_coarse):
                column = up(c, d, n_coarse) * LOW
                for part in range(LOW):
                    arrival(column + part).wait_recv()

        def sent():
            low().wait_send()
            for d in range(1, n_coarse):
                far(d, False).wait_send()
                far(d, True).wait_send()

        return begin, relay, arrive, sent

    enc_plane = plane(encbuf.at[me_kv], encbuf, ek_s, ek_r)
    dec_plane = plane(dec.at[me_kv], dec, dk_s, dk_r)
    k_plane = plane(kh, kbuf, k_s, k_r)
    v_plane = plane(vh, vbuf, v_s, v_r)

    def o_copy(d):
        peer = up(me_q, d, n_q)
        return (
            remote(osend.at[peer], orecv.at[me_q], o_s.at[d], o_r.at[me_q], at_q(peer)),
            remote(ssend.at[peer], srecv.at[me_q], st_s.at[d], st_r.at[me_q], at_q(peer)),
        )

    def o_arrival(d):
        src = down(me_q, d, n_q)
        return (
            remote(osend.at[src], orecv.at[src], o_s.at[d], o_r.at[src], at_q(src)),
            remote(ssend.at[src], srecv.at[src], st_s.at[d], st_r.at[src], at_q(src)),
        )

    def halo_copy(side):
        peer = jnp.clip(here + 1 - 2 * side, 0, n_seq - 1)
        return (
            remote(kl, khalo.at[side], h_s.at[side, 0], h_r.at[side, 0], at_seq(peer)),
            remote(vl, vhalo.at[side], h_s.at[side, 1], h_r.at[side, 1], at_seq(peer)),
        )

    def loop(start, stop, body):
        def step(d, carry):
            body(d)
            return carry
        lax.fori_loop(start, stop, step, 0)

    for d in range(1, n_q):
        enc_copy(d).start()
    k_plane[0]()
    has_up = me_q < n_q - 1
    has_down = me_q > 0

    @pl.when(has_up)
    def _():
        own_q(1).start()

    @pl.when(has_down)
    def _():
        own_q(-1).start()

    has_next = here < n_seq - 1
    has_prev = here > 0

    encbuf[me_kv, me_q] = enc[...]
    for d in range(1, n_q):
        enc_arrival(d).wait_recv()
    enc_plane[0]()
    v_plane[0]()

    @pl.when(has_next)
    def _():
        for copy in halo_copy(0):
            copy.start()

    @pl.when(has_prev)
    def _():
        for copy in halo_copy(1):
            copy.start()

    qbuf[me_q] = qh[...]
    kbuf[me_kv] = kh[...]
    vbuf[me_kv] = vh[...]
    row = lax.broadcasted_iota(jnp.int32, (tokens, 3 * tokens), 0)
    col = lax.broadcasted_iota(jnp.int32, (tokens, 3 * tokens), 1)
    pos = here * tokens + col - tokens
    seen = (jnp.abs(col - tokens - row) <= ROUTED_BLOCK - 1) & (pos >= 0) & (pos < n_seq * tokens)
    band[...] = jnp.where(seen, jnp.float32(0), jnp.float32(NEG))

    load.wait()
    lane_d = lax.broadcasted_iota(jnp.int32, (dec_rows, PAIR), 1)
    for j in range(pairs):
        q = drows[:, j * PAIR:(j + 1) * PAIR].astype(jnp.float32) * (HEAD ** (-0.5))
        swapped = pltpu.roll(q, HEAD, 1)
        both = jnp.concatenate(
            [jnp.where(lane_d < HEAD, q, 0.0), jnp.where(lane_d < HEAD, swapped, 0.0)], axis=0
        )
        dq[2 * j * dec_rows:(2 * j + 2) * dec_rows, :] = both.astype(jnp.bfloat16)
    q_step(1)
    enc_plane[1]()
    k_plane[1]()
    v_plane[1]()

    for t in range(2, n_q - 1):
        q_step(t)
    enc_plane[2]()
    d_total = heads * dec_rows
    d_chunk = min(256, d_total)

    def dec_step(i):
        rows = pl.ds(pl.multiple_of(i * d_chunk, d_chunk), d_chunk)
        kv = encbuf[...].reshape(n_seq * tokens, PAIR)
        s = dot_t(dq[rows, :], kv)
        p = jnp.exp(s - jnp.max(s, axis=1, keepdims=True))
        total = jnp.sum(p, axis=1, keepdims=True)
        do[rows, :] = dot(p.astype(jnp.bfloat16), kv) / total

    loop(0, d_total // d_chunk, dec_step)
    for j in range(pairs):
        even = do[2 * j * dec_rows:(2 * j + 1) * dec_rows, :]
        odd = do[(2 * j + 1) * dec_rows:(2 * j + 2) * dec_rows, :]
        dec[me_kv, me_q, :, j * PAIR:(j + 1) * PAIR] = jnp.where(
            lane_d < HEAD, pltpu.roll(even, HEAD, 1), odd
        ).astype(jnp.bfloat16)
    for d in range(1, n_q):
        dec_copy(d).start()

    low_half = lax.broadcasted_iota(jnp.int32, (tokens, PAIR), 1) < HEAD
    lane = lax.broadcasted_iota(jnp.int32, (tokens, PAIR), 1)
    if n_q > 2:
        q_step(n_q - 1)
    for d in range(1, n_q):
        dec_arrival(d).wait_recv()
    dec_plane[0]()
    k_plane[2]()
    v_plane[2]()
    for d in list(range(1, n_q)) + [0]:
        block = up(me_q, d, n_q)
        if d == 0:
            dec_plane[1]()

        def pair_step(j, stat):
            cols = pl.ds(pl.multiple_of(j * PAIR, PAIR), PAIR)
            q = stacked_pair(qbuf[block, :, cols], low_half)
            s = dot_t(q, kbuf[:, :, cols].reshape(n_kv * tokens, PAIR))
            if has_bias:
                s = s + bias_ref[0:1, :]
            peak = jnp.max(s, axis=1, keepdims=True)
            p = jnp.exp(s - peak)
            total = jnp.sum(p, axis=1, keepdims=True)
            o = dot(p.astype(jnp.bfloat16), vbuf[:, :, cols].reshape(n_kv * tokens, PAIR)) / total
            lse = peak + jnp.log(total)
            osend[block, :, cols] = jnp.where(low_half, o[:tokens], o[tokens:]).astype(jnp.bfloat16)
            stat = jnp.where(lane == 2 * j, lse[:tokens], stat)
            return jnp.where(lane == 2 * j + 1, lse[tokens:], stat)

        stat = lax.fori_loop(0, pairs, pair_step, jnp.zeros((tokens, PAIR), jnp.float32))
        ssend[block] = stat.T[:heads]
        if d:
            for copy in o_copy(d):
                copy.start()
        else:
            wts[0] = stat

    @pl.when(has_prev)
    def _():
        for copy in halo_copy(0):
            copy.wait_recv()

    @pl.when(jnp.logical_not(has_prev))
    def _():
        khalo[0] = jnp.zeros_like(kl)
        vhalo[0] = jnp.zeros_like(vl)

    @pl.when(has_next)
    def _():
        for copy in halo_copy(1):
            copy.wait_recv()

    @pl.when(jnp.logical_not(has_next))
    def _():
        khalo[1] = jnp.zeros_like(kl)
        vhalo[1] = jnp.zeros_like(vl)

    def light_step(j):
        cols = pl.ds(pl.multiple_of(j * PAIR, PAIR), PAIR)
        q = stacked_pair(ql[:, cols], low_half)
        keys = jnp.concatenate([khalo[0, :, cols], kl[:, cols], khalo[1, :, cols]], axis=0)
        rows = jnp.concatenate([vhalo[0, :, cols], vl[:, cols], vhalo[1, :, cols]], axis=0)
        mask = band[...]
        s = dot_t(q, keys) + jnp.concatenate([mask, mask], axis=0)
        p = jnp.exp(s - jnp.max(s, axis=1, keepdims=True))
        total = jnp.sum(p, axis=1, keepdims=True)
        o = dot(p.astype(jnp.bfloat16), rows) / total
        light[:, cols] = jnp.where(low_half, o[:tokens], o[tokens:])

    loop(0, pairs, light_step)

    for d in range(1, n_q):
        for copy in o_arrival(d):
            copy.wait_recv()
        pad = jnp.zeros((PAIR - heads, tokens), jnp.float32)
        wts[d] = jnp.concatenate([srecv[down(me_q, d, n_q)], pad], axis=0).T
    top = wts[0]
    for d in range(1, n_q):
        top = jnp.maximum(top, wts[d])
    norm = jnp.zeros_like(top)
    for d in range(n_q):
        share = jnp.exp(wts[d] - top)
        wts[d] = share
        norm = norm + share
    for d in range(n_q):
        wts[d] = wts[d] / norm

    def join_step(j):
        cols = pl.ds(pl.multiple_of(j * PAIR, PAIR), PAIR)
        acc = jnp.zeros((tokens, PAIR), jnp.float32)
        for d in range(n_q):
            part = osend[me_q, :, cols] if d == 0 else orecv[down(me_q, d, n_q), :, cols]
            w = wts[d]
            even = jnp.sum(jnp.where(lane == 2 * j, w, 0.0), axis=1, keepdims=True)
            odd = jnp.sum(jnp.where(lane == 2 * j + 1, w, 0.0), axis=1, keepdims=True)
            acc = acc + jnp.where(low_half, even, odd) * part.astype(jnp.float32)
        heavy = acc.astype(jnp.bfloat16).astype(jnp.float32)
        out[:, cols] = (light[:, cols] + heavy).astype(jnp.bfloat16)

    loop(0, pairs, join_step)

    dec_plane[2]()
    for part in (enc_plane, dec_plane, k_plane, v_plane):
        part[3]()
    for d in range(1, n_q):
        enc_copy(d).wait_send()
        dec_copy(d).wait_send()
        for copy in o_copy(d):
            copy.wait_send()

    @pl.when(has_up)
    def _():
        own_q(1).wait_send()

    @pl.when(has_down)
    def _():
        own_q(-1).wait_send()

    for t in range(1, n_q - 1):
        for way in (1, -1):
            src = me_q - way * t

            @pl.when((src >= 0) & (src < n_q) & (me_q + way >= 0) & (me_q + way < n_q))
            def _():
                q_copy(jnp.clip(src, 0, n_q - 1), way).wait_send()

    @pl.when(has_next)
    def _():
        for copy in halo_copy(0):
            copy.wait_send()

    @pl.when(has_prev)
    def _():
        for copy in halo_copy(1):
            copy.wait_send()


def local(
    q_light, k_light, v_light, q_heavy, k_heavy, v_heavy, enc_kv, dec_queries, query_ids, key_ids
):
    _, tokens, width = q_light.shape
    n_coarse = lax.axis_size("coarse")
    n_fine = lax.axis_size("fine")
    n_seq = n_coarse * n_fine
    n_q = n_fine // LOW
    n_kv = n_coarse * LOW
    heads = width // HEAD
    count = dec_queries.shape[1]
    dec_rows = count // n_seq
    mine = dec_queries.reshape(n_kv, n_q, dec_rows, width)
    args = [q_light[0], k_light[0], v_light[0], q_heavy[0], k_heavy[0], v_heavy[0], enc_kv[0], mine]
    has_bias = key_ids.shape[1] != n_seq
    if has_bias:
        high = lax.div(lax.axis_index("fine"), LOW)
        member = jnp.arange(n_kv, dtype=jnp.int32)
        blocks = (member // LOW) * n_fine + high * LOW + member % LOW
        listed = jnp.any(blocks[:, None] == key_ids[0][None, :], axis=1)
        bias = jnp.repeat(jnp.where(listed, 0.0, NEG).astype(jnp.float32), tokens)
        args.append(jnp.broadcast_to(bias[None], (8, n_kv * tokens)))
    bf16, f32 = jnp.bfloat16, jnp.float32
    dma = pltpu.SemaphoreType.DMA
    vmem = pl.BlockSpec(memory_space=pltpu.VMEM)
    encoded, decoded = pl.pallas_call(
        functools.partial(kernel, (n_coarse, n_fine, tokens, width, dec_rows), has_bias),
        out_shape=(
            jax.ShapeDtypeStruct((tokens, width), bf16),
            jax.ShapeDtypeStruct((n_kv, n_q, dec_rows, width), bf16),
        ),
        in_specs=[vmem] * 7 + [pl.BlockSpec(memory_space=pl.ANY)] + [vmem] * (len(args) - 8),
        out_specs=(vmem, vmem),
        scratch_shapes=[
            pltpu.VMEM((n_kv, n_q, tokens, PAIR), bf16),
            pltpu.VMEM((heads * dec_rows, PAIR), bf16),
            pltpu.VMEM((heads * dec_rows, PAIR), f32),
            pltpu.VMEM((n_q, tokens, width), bf16),
            pltpu.VMEM((n_kv, tokens, width), bf16),
            pltpu.VMEM((n_kv, tokens, width), bf16),
            pltpu.VMEM((2, tokens, width), bf16),
            pltpu.VMEM((2, tokens, width), bf16),
            pltpu.VMEM((n_q, tokens, width), bf16),
            pltpu.VMEM((n_q, tokens, width), bf16),
            pltpu.VMEM((n_q, heads, tokens), f32),
            pltpu.VMEM((n_q, heads, tokens), f32),
            pltpu.VMEM((n_q, tokens, PAIR), f32),
            pltpu.VMEM((tokens, width), f32),
            pltpu.VMEM((tokens, 3 * tokens), f32),
            dma((n_q,)), dma((n_q,)),
            dma((n_q,)), dma((n_q,)),
            dma((n_q + 2,)), dma((n_q,)),
            dma((n_q,)), dma((n_q,)),
            dma((n_q,)), dma((n_q,)),
            dma((2, 2)), dma((2, 2)),
            dma((2, n_coarse)), dma((n_kv,)),
            dma((2, n_coarse)), dma((n_kv,)),
            dma((2, n_coarse)), dma((n_kv,)),
            dma((2, n_coarse)), dma((n_kv,)),
            pltpu.VMEM((dec_rows, width), bf16), dma,
        ],
        compiler_params=pltpu.CompilerParams(
            collective_id=0, has_side_effects=True, vmem_limit_bytes=60 * 1024 * 1024
        ),
    )(*args)
    return encoded[None], decoded.reshape(1, count, width)


def solution(mesh):
    rows = P("doc", ("coarse", "fine"), None)
    placed = (rows,) * 7 + (P("doc", None, None), P("doc", None), P("doc", None))
    return jax.shard_map(
        local,
        mesh=mesh,
        in_specs=placed,
        out_specs=(rows, P("doc", None, None)),
        check_vma=False,
    )
```

profile of v0, /device:TPU:0, one launch (start us, length us, event | category | flops | bytes accessed | tf_op | source)
XLA Modules:
  0.0 78.5 jit_solution(11207994403442865562)
XLA Ops:
  0.6 73.9 %shard_map.95 = (bf16[128,1024]{1,0:T(8,128)(2,1)}, bf16[4,4,32,1024]{3,2,1,0:T(8,128)(2,1)}) custom-call(bf16[128,1024]{1,0:T(8,128)(2,1)} %bitcast.13, bf16[128,1024]{1,0:T(8,128)(2,1)} %bitcast.14, bf16[128,1024]{1,0:T(8,128)(2,1)} %bitcast.15, bf16[128,1024]{1,0:T(8,128)(2,1)} %bitcast.16, bf16[128,1024]{1,0:T(8,128)(2,1)} %bitcast.17, ...), custom_call_target="tpu_custom_call" | custom-call | tf_op jit(solution)/shard_map/pallas_call | solution.py:437
  74.5 1.7 %copy.12 = bf16[1,128,1024]{2,1,0:T(8,128)(2,1)} copy(bf16[1,128,1024]{2,1,0:T(8,128)(2,1)} %bitcast.12) | data formatting | bytes 524288
  76.2 2.3 %copy.13 = bf16[1,512,1024]{2,1,0:T(8,128)(2,1)} copy(bf16[1,512,1024]{2,1,0:T(8,128)(2,1)} %bitcast.10) | data formatting | bytes 2097152
where the time goes:
time: 79.5 us; the launch traced here: 78.5 us
  Pallas kernels  73.9 us (93%)
  local copies, waits for them, and re-layouts  3.93 us (5%)
    pallas_call x1, Pallas kernels, local(): pl.pallas_call(functools.partial(kernel, (n_coarse, n_fine, tokens, width...  73.9 us
    unnamed x2, local copies, waits for them, and re-layouts  3.93 us

commit v1 on v0

v1 whole, which is shorter than its diff:
```python
import functools

import jax
import jax.numpy as jnp
from jax import lax
from jax.experimental import pallas as pl
from jax.experimental.pallas import tpu as pltpu
from jax.sharding import PartitionSpec as P

HEAD = 64
PAIR = 2 * HEAD
ROUTED_BLOCK = 128
LOW = 2
MESH = pl.DeviceIdType.MESH
NEG = -1e30


def dot_t(a, b):
    return lax.dot_general(a, b, (((1,), (1,)), ((), ())), preferred_element_type=jnp.float32)


def dot(a, b):
    return jnp.dot(a, b, preferred_element_type=jnp.float32)


def stacked_pair(q, low_half):
    q = q * jnp.asarray(HEAD ** (-0.5), q.dtype)
    zero = jnp.zeros_like(q)
    return jnp.concatenate([jnp.where(low_half, q, zero), jnp.where(low_half, zero, q)], axis=0)


def flip(v, d, n):
    out, bit = 0, 1
    while bit < n:
        if isinstance(d, int):
            on = (d // bit) % 2
        else:
            on = lax.rem(lax.div(d, bit), 2)
        out = out + lax.rem(lax.div(v, bit) + on, 2) * bit
        bit *= 2
    return out


def kernel(dims, has_bias, *refs):
    n_coarse, n_fine, tokens, width, dec_rows = dims
    n_seq = n_coarse * n_fine
    n_q = n_fine // LOW
    n_kv = n_coarse * LOW
    n_pair_seq = n_seq // LOW
    half = n_fine // 2
    heads = width // HEAD
    pairs = heads // 2
    share = n_fine // pairs
    wide = width // LOW
    pairs_half = pairs // LOW
    refs = list(refs)
    ql, kl, vl, qh, kh, vh, enc, decq = refs[:8]
    bias_ref = refs[8] if has_bias else None
    (out, dec, encbuf, drows, dq, do, qbuf, kbuf, vbuf, acc, stat, osend, orecv,
     lq, lk, lv, lown, lsend, lrecv, band,
     load_s, enc_s, enc_r, ek_s, ek_r, q_s, q_r, k_s, k_r, v_s, v_r, kx_s, vx_s,
     x_s, x_r, h_s, h_r, o_s, o_r, lo_s, lo_r, dec_s, dec_r) = refs[8 + has_bias:]

    c = lax.axis_index("coarse")
    f = lax.axis_index("fine")
    here = c * n_fine + f
    me_q = lax.div(f, LOW)
    lo = lax.rem(f, LOW)
    me_kv = c * LOW + lo
    p = lax.div(f, share)
    s_me = lax.rem(f, share)
    hh = lax.div(f, half)
    g = lax.rem(f, half)
    two = lax.div(here, LOW)

    def remote(src, dst, ssem, rsem, device):
        return pltpu.make_async_remote_copy(
            src_ref=src, dst_ref=dst, send_sem=ssem, recv_sem=rsem,
            device_id=device, device_id_type=MESH,
        )

    def up(me, d, n):
        return lax.rem(me + d, n)

    def down(me, d, n):
        return lax.rem(me + n - d, n)

    def at(cc, ff):
        return {"coarse": cc, "fine": ff}

    def cols_of(pair):
        return pl.ds(pl.multiple_of(pair * PAIR, PAIR), PAIR)

    def side_of(which):
        return pl.ds(pl.multiple_of(which * wide, PAIR), wide)

    def loop(start, stop, body):
        def step(d, carry):
            body(d)
            return carry
        lax.fori_loop(start, stop, step, 0)

    loads = [
        pltpu.make_async_copy(enc, encbuf.at[me_kv, me_q], load_s.at[0]),
        pltpu.make_async_copy(kh.at[:, cols_of(p)], kbuf.at[c, f], load_s.at[1]),
        pltpu.make_async_copy(vh.at[:, cols_of(p)], vbuf.at[c, f], load_s.at[2]),
        pltpu.make_async_copy(qh.at[:, cols_of(p)], qbuf.at[p], load_s.at[3]),
        pltpu.make_async_copy(decq.at[c, g], drows, load_s.at[4]),
        pltpu.make_async_copy(kl.at[:, side_of(lo)], lk.at[1 + lo], load_s.at[5]),
        pltpu.make_async_copy(vl.at[:, side_of(lo)], lv.at[1 + lo], load_s.at[6]),
        pltpu.make_async_copy(ql.at[:, side_of(lo)], lq.at[lo], load_s.at[7]),
    ]
    for copy in loads:
        copy.start()

    barrier = pltpu.get_barrier_semaphore()

    def greet(d, carry):
        t = up(here, d, n_seq)
        pl.semaphore_signal(
            barrier, inc=1, device_id=at(lax.div(t, n_fine), lax.rem(t, n_fine)), device_id_type=MESH
        )
        return carry

    lax.fori_loop(1, n_seq, greet, 0)
    pl.semaphore_wait(barrier, n_seq - 1)

    def at_q(a):
        return at(c, a * LOW + lo)

    def at_kv(b):
        return at(lax.div(b, LOW), me_q * LOW + lax.rem(b, LOW))

    def enc_copy(d):
        return remote(enc, encbuf.at[me_kv, me_q], enc_s.at[d], enc_r.at[me_q], at_q(up(me_q, d, n_q)))

    def enc_arrival(d):
        src = down(me_q, d, n_q)
        return remote(enc, encbuf.at[me_kv, src], enc_s.at[d], enc_r.at[src], at_q(src))

    other = c * LOW + 1 - lo

    def enc_low():
        return remote(encbuf.at[me_kv], encbuf.at[me_kv], ek_s.at[0, 0], ek_r.at[me_kv], at_kv(other))

    def enc_far(d, relay):
        block = other if relay else me_kv
        peer = up(c, d, n_coarse) * LOW + lo
        return remote(encbuf.at[block], encbuf.at[block], ek_s.at[int(relay), d], ek_r.at[block], at_kv(peer))

    def enc_block(block):
        return remote(encbuf.at[block], encbuf.at[block], ek_s.at[0, 0], ek_r.at[block], at_kv(block))

    def q_copy(d):
        to = flip(p, d, pairs)
        return remote(qh.at[:, cols_of(to)], qbuf.at[p], q_s.at[d], q_r.at[p], at(c, to * share + s_me))

    def q_arrival(d):
        src = flip(p, d, pairs)
        return remote(qbuf.at[src], qbuf.at[src], q_s.at[d], q_r.at[src], at(c, src * share + s_me))

    def kv_copy(d):
        to = flip(f, d, n_fine)
        col = cols_of(lax.div(to, share))
        return (
            remote(kh.at[:, col], kbuf.at[c, f], k_s.at[d], k_r.at[c, f], at(c, to)),
            remote(vh.at[:, col], vbuf.at[c, f], v_s.at[d], v_r.at[c, f], at(c, to)),
        )

    def kv_block(cc, ff):
        return (
            remote(kbuf.at[cc, ff], kbuf.at[cc, ff], k_s.at[0], k_r.at[cc, ff], at(cc, ff)),
            remote(vbuf.at[cc, ff], vbuf.at[cc, ff], v_s.at[0], v_r.at[cc, ff], at(cc, ff)),
        )

    def kv_relay(d, e):
        src = flip(f, d, n_fine)
        peer = at(up(c, e, n_coarse), f)
        return (
            remote(kbuf.at[c, src], kbuf.at[c, src], kx_s.at[d, e], k_r.at[c, src], peer),
            remote(vbuf.at[c, src], vbuf.at[c, src], vx_s.at[d, e], v_r.at[c, src], peer),
        )

    def kv_forward(d):
        if d:
            for copy in kv_block(c, flip(f, d, n_fine)):
                copy.wait_recv()
        for e in range(1, n_coarse):
            for copy in kv_relay(d, e):
                copy.start()

    def o_copy(d):
        to = flip(p, d, pairs)
        return remote(osend.at[to], orecv.at[p], o_s.at[d], o_r.at[p], at(c, to * share + s_me))

    def o_arrival(d):
        src = flip(p, d, pairs)
        return remote(osend.at[src], orecv.at[src], o_s.at[d], o_r.at[src], at(c, src * share + s_me))

    mate = at(c, f + 1 - 2 * lo)

    def swap_copy():
        cols = side_of(1 - lo)
        return (
            remote(kl.at[:, cols], lk.at[1 + lo], x_s.at[0], x_r.at[0], mate),
            remote(vl.at[:, cols], lv.at[1 + lo], x_s.at[1], x_r.at[1], mate),
            remote(ql.at[:, cols], lq.at[lo], x_s.at[2], x_r.at[2], mate),
        )

    def swap_arrival():
        return (
            remote(lk.at[2 - lo], lk.at[2 - lo], x_s.at[0], x_r.at[0], mate),
            remote(lv.at[2 - lo], lv.at[2 - lo], x_s.at[1], x_r.at[1], mate),
            remote(lq.at[1 - lo], lq.at[1 - lo], x_s.at[2], x_r.at[2], mate),
        )

    def halo_copy(side):
        peer = jnp.clip(two + 2 * side - 1, 0, n_pair_seq - 1) * LOW + lo
        device = at(lax.div(peer, n_fine), lax.rem(peer, n_fine))
        slot = 3 - 3 * side
        return (
            remote(lk.at[1 + side], lk.at[slot], h_s.at[side, 0], h_r.at[side, 0], device),
            remote(lv.at[1 + side], lv.at[slot], h_s.at[side, 1], h_r.at[side, 1], device),
        )

    has_peer = [two > 0, two < n_pair_seq - 1]

    def light_back():
        return remote(lsend, lrecv, lo_s, lo_r, mate)

    bits = []
    bit = half // 2
    while bit:
        bits.append(bit)
        bit //= 2

    def dec_copy(block, k):
        mine = dec.at[c, block]
        if k < len(bits):
            peer = at(c, hh * half + flip(g, bits[k], half))
        else:
            peer = at(up(c, k - len(bits) + 1, n_coarse), f)
        return remote(mine, mine, dec_s.at[k, block], dec_r.at[c, block], peer)

    def dec_arrival(cc, block):
        part = dec.at[cc, block]
        return remote(part, part, dec_s.at[0, 0], dec_r.at[cc, block], at(cc, f))

    def dec_spread(block, first):
        for k in range(first, len(bits) + n_coarse - 1):
            dec_copy(block, k).start()

    def dec_stage(k):
        done = [0]
        for b in bits[:k]:
            done = done + [x + b for x in done]
        return [flip(g, x + bits[k], half) for x in done]

    def dec_forward(k):
        for block in dec_stage(k):
            dec_arrival(c, block).wait_recv()
            dec_spread(block, k + 1)

    for d in range(1, n_q):
        enc_copy(d).start()
    for d in range(1, pairs):
        q_copy(d).start()
    loads[1].wait()
    loads[2].wait()
    kv_forward(0)
    for d in range(1, n_fine):
        for copy in kv_copy(d):
            copy.start()
    for copy in swap_copy():
        copy.start()
    loads[5].wait()
    loads[6].wait()

    for side in range(2):
        @pl.when((lo == side) & has_peer[side])
        def _():
            for copy in halo_copy(side):
                copy.start()

    row = lax.broadcasted_iota(jnp.int32, (tokens, 3 * tokens), 0)
    col = lax.broadcasted_iota(jnp.int32, (tokens, 3 * tokens), 1)
    for b in range(LOW):
        pos = (two * LOW + b) * tokens + col - tokens
        seen = (jnp.abs(col - tokens - row) <= ROUTED_BLOCK - 1) & (pos >= 0) & (pos < n_seq * tokens)
        band[b] = jnp.where(seen, jnp.float32(0), jnp.float32(NEG))

    loads[4].wait()
    lane_d = lax.broadcasted_iota(jnp.int32, (dec_rows, PAIR), 1)
    for j in range(pairs):
        q = drows[:, j * PAIR:(j + 1) * PAIR].astype(jnp.float32) * (HEAD ** (-0.5))
        swapped = pltpu.roll(q, HEAD, 1)
        both = jnp.concatenate(
            [jnp.where(lane_d < HEAD, q, 0.0), jnp.where(lane_d < HEAD, swapped, 0.0)], axis=0
        )
        dq[2 * j * dec_rows:(2 * j + 2) * dec_rows, :] = both.astype(jnp.bfloat16)

    loads[0].wait()
    for d in range(1, n_q):
        enc_arrival(d).wait_recv()
    enc_low().start()
    for d in range(1, n_coarse):
        enc_far(d, False).start()
    enc_block(other).wait_recv()
    for d in range(1, n_coarse):
        enc_far(d, True).start()

    for d in range(1, half):
        kv_forward(d)

    for d in range(1, n_coarse):
        for part in range(LOW):
            enc_block(up(c, d, n_coarse) * LOW + part).wait_recv()

    d_total = heads * dec_rows
    d_chunk = min(256, d_total)

    def dec_step(i):
        rows = pl.ds(pl.multiple_of(i * d_chunk, d_chunk), d_chunk)
        kv = encbuf[...].reshape(n_seq * tokens, PAIR)
        s = dot_t(dq[rows, :], kv)
        e = jnp.exp(s - jnp.max(s, axis=1, keepdims=True))
        total = jnp.sum(e, axis=1, keepdims=True)
        do[rows, :] = dot(e.astype(jnp.bfloat16), kv) / total

    loop(0, d_total // d_chunk, dec_step)
    for j in range(pairs):
        even = do[2 * j * dec_rows:(2 * j + 1) * dec_rows, :]
        odd = do[(2 * j + 1) * dec_rows:(2 * j + 2) * dec_rows, :]
        dec[c, g, :, j * PAIR:(j + 1) * PAIR] = jnp.where(
            lane_d < HEAD, pltpu.roll(even, HEAD, 1), odd
        ).astype(jnp.bfloat16)
    dec_spread(g, 0)

    low_half = lax.broadcasted_iota(jnp.int32, (tokens, PAIR), 1) < HEAD
    lane_2 = lax.broadcasted_iota(jnp.int32, (2 * tokens, PAIR), 1)
    keys = n_coarse * half * tokens

    def heavy_scores(j, part):
        q = stacked_pair(qbuf[j], low_half)
        s = dot_t(q, kbuf[:, pl.ds(part * half, half)].reshape(keys, PAIR))
        if has_bias:
            s = s + bias_ref[part, 0:1, :]
        return s

    def heavy_values(part):
        return vbuf[:, pl.ds(part * half, half)].reshape(keys, PAIR)

    def heavy_first(j):
        s = heavy_scores(j, hh)
        peak = jnp.max(s, axis=1, keepdims=True)
        e = jnp.exp(s - peak)
        total = jnp.sum(e, axis=1, keepdims=True)
        acc[j] = dot(e.astype(jnp.bfloat16), heavy_values(hh))
        stat[j] = jnp.where(lane_2 == 0, peak, total)

    def heavy_second(j):
        s = heavy_scores(j, 1 - hh)
        before = stat[j, :, 0:1]
        peak = jnp.maximum(before, jnp.max(s, axis=1, keepdims=True))
        e = jnp.exp(s - peak)
        keep = jnp.exp(before - peak)
        total = stat[j, :, 1:2] * keep + jnp.sum(e, axis=1, keepdims=True)
        o = (acc[j] * keep + dot(e.astype(jnp.bfloat16), heavy_values(1 - hh))) / total
        return jnp.where(low_half, o[:tokens], o[tokens:]).astype(jnp.bfloat16)

    loads[3].wait()
    for d in range(1, pairs):
        q_arrival(d).wait_recv()
    for e in range(1, n_coarse):
        for i in range(half):
            for copy in kv_block(up(c, e, n_coarse), hh * half + i):
                copy.wait_recv()
    per = max(1, pairs // half)
    done = 0
    for r in range(half):
        stop = pairs if r == half - 1 else min(pairs, done + per)
        loop(done, stop, heavy_first)
        done = stop
        kv_forward(half + r)

    for k in range(len(bits) - 1):
        dec_forward(k)
    arrived = swap_arrival()
    arrived[0].wait_recv()
    arrived[1].wait_recv()
    for side in range(2):
        @pl.when((lo == 1 - side) & has_peer[side])
        def _():
            for copy in halo_copy(side):
                copy.start()

    for e in range(1, n_coarse):
        for i in range(half):
            for copy in kv_block(up(c, e, n_coarse), (1 - hh) * half + i):
                copy.wait_recv()

    def heavy_out(i):
        d = pairs - 1 - i
        j = flip(p, d, pairs)
        osend[j] = heavy_second(j)
        o_copy(d).start()

    loop(0, pairs - 1, heavy_out)
    orecv[p] = heavy_second(p)
    dec_forward(len(bits) - 1)

    arrived[2].wait_recv()
    loads[7].wait()
    for side in range(2):
        @pl.when(has_peer[side])
        def _():
            for copy in halo_copy(1 - side):
                copy.wait_recv()

        @pl.when(jnp.logical_not(has_peer[side]))
        def _():
            lk[3 * side] = jnp.zeros((tokens, wide), jnp.bfloat16)
            lv[3 * side] = jnp.zeros((tokens, wide), jnp.bfloat16)

    def light_of(b, j):
        cols = cols_of(j)
        q = stacked_pair(lq[b, :, cols], low_half)
        mask = band[b]
        s = dot_t(q, lk[pl.ds(b, 3), :, cols].reshape(3 * tokens, PAIR))
        s = s + jnp.concatenate([mask, mask], axis=0)
        e = jnp.exp(s - jnp.max(s, axis=1, keepdims=True))
        total = jnp.sum(e, axis=1, keepdims=True)
        o = dot(e.astype(jnp.bfloat16), lv[pl.ds(b, 3), :, cols].reshape(3 * tokens, PAIR)) / total
        return jnp.where(low_half, o[:tokens], o[tokens:])

    def light_away(j):
        lsend[:, cols_of(j)] = light_of(1 - lo, j).astype(jnp.bfloat16)

    def light_home(j):
        lown[:, cols_of(j)] = light_of(lo, j)

    loop(0, pairs_half, light_away)
    light_back().start()
    loop(0, pairs_half, light_home)

    for d in range(1, pairs):
        o_arrival(d).wait_recv()

    def join_home(j):
        pair = lo * pairs_half + j
        heavy = orecv[pair].astype(jnp.float32)
        out[:, cols_of(pair)] = (lown[:, cols_of(j)] + heavy).astype(jnp.bfloat16)

    def join_away(j):
        pair = (1 - lo) * pairs_half + j
        heavy = orecv[pair].astype(jnp.float32)
        out[:, cols_of(pair)] = (lrecv[:, cols_of(j)].astype(jnp.float32) + heavy).astype(jnp.bfloat16)

    loop(0, pairs_half, join_home)
    light_back().wait_recv()
    loop(0, pairs_half, join_away)

    for e in range(1, n_coarse):
        for block in range(half):
            dec_arrival(up(c, e, n_coarse), block).wait_recv()
    for d in range(1, n_q):
        enc_copy(d).wait_send()
    enc_low().wait_send()
    for d in range(1, n_coarse):
        enc_far(d, False).wait_send()
        enc_far(d, True).wait_send()
    for d in range(1, pairs):
        q_copy(d).wait_send()
        o_copy(d).wait_send()
    for d in range(n_fine):
        if d:
            for copy in kv_copy(d):
                copy.wait_send()
        for e in range(1, n_coarse):
            for copy in kv_relay(d, e):
                copy.wait_send()
    for copy in swap_copy():
        copy.wait_send()
    light_back().wait_send()
    for side in range(2):
        @pl.when(has_peer[side])
        def _():
            for copy in halo_copy(side):
                copy.wait_send()
    for k in range(len(bits) + n_coarse - 1):
        sent = [0]
        for b in bits[:k]:
            sent = sent + [x + b for x in sent]
        for x in sent:
            dec_copy(flip(g, x, half), k).wait_send()


def local(
    q_light, k_light, v_light, q_heavy, k_heavy, v_heavy, enc_kv, dec_queries, query_ids, key_ids
):
    _, tokens, width = q_light.shape
    n_coarse = lax.axis_size("coarse")
    n_fine = lax.axis_size("fine")
    n_seq = n_coarse * n_fine
    n_q = n_fine // LOW
    n_kv = n_coarse * LOW
    half = n_fine // 2
    heads = width // HEAD
    pairs = heads // 2
    count = dec_queries.shape[1]
    dec_rows = count // (n_coarse * half)
    n_bits = half.bit_length() - 1
    mine = dec_queries.reshape(n_coarse, half, dec_rows, width)
    args = [q_light[0], k_light[0], v_light[0], q_heavy[0], k_heavy[0], v_heavy[0], enc_kv[0], mine]
    has_bias = key_ids.shape[1] != n_seq
    keys = n_coarse * half * tokens
    if has_bias:
        blocks = jnp.arange(n_seq, dtype=jnp.int32).reshape(n_coarse, 2, half).transpose(1, 0, 2)
        listed = jnp.any(blocks[..., None] == key_ids[0], axis=-1).reshape(2, 1, n_coarse * half)
        bias = jnp.repeat(jnp.where(listed, 0.0, NEG).astype(jnp.float32), tokens, axis=2)
        args.append(jnp.broadcast_to(bias, (2, 8, keys)))
    bf16, f32 = jnp.bfloat16, jnp.float32
    dma = pltpu.SemaphoreType.DMA
    vmem = pl.BlockSpec(memory_space=pltpu.VMEM)
    hbm = pl.BlockSpec(memory_space=pltpu.HBM)
    wide = width // LOW
    encoded, decoded = pl.pallas_call(
        functools.partial(kernel, (n_coarse, n_fine, tokens, width, dec_rows), has_bias),
        out_shape=(
            jax.ShapeDtypeStruct((tokens, width), bf16),
            jax.ShapeDtypeStruct((n_coarse, half, dec_rows, width), bf16),
        ),
        in_specs=[hbm] * 8 + [vmem] * (len(args) - 8),
        out_specs=(vmem, vmem),
        scratch_shapes=[
            pltpu.VMEM((n_kv, n_q, tokens, PAIR), bf16),
            pltpu.VMEM((dec_rows, width), bf16),
            pltpu.VMEM((heads * dec_rows, PAIR), bf16),
            pltpu.VMEM((heads * dec_rows, PAIR), f32),
            pltpu.VMEM((pairs, tokens, PAIR), bf16),
            pltpu.VMEM((n_coarse, n_fine, tokens, PAIR), bf16),
            pltpu.VMEM((n_coarse, n_fine, tokens, PAIR), bf16),
            pltpu.VMEM((pairs, 2 * tokens, PAIR), f32),
            pltpu.VMEM((pairs, 2 * tokens, PAIR), f32),
            pltpu.VMEM((pairs, tokens, PAIR), bf16),
            pltpu.VMEM((pairs, tokens, PAIR), bf16),
            pltpu.VMEM((2, tokens, wide), bf16),
            pltpu.VMEM((4, tokens, wide), bf16),
            pltpu.VMEM((4, tokens, wide), bf16),
            pltpu.VMEM((tokens, wide), f32),
            pltpu.VMEM((tokens, wide), bf16),
            pltpu.VMEM((tokens, wide), bf16),
            pltpu.VMEM((2, tokens, 3 * tokens), f32),
            dma((8,)),
            dma((n_q,)), dma((n_q,)),
            dma((2, n_coarse)), dma((n_kv,)),
            dma((pairs,)), dma((pairs,)),
            dma((n_fine,)), dma((n_coarse, n_fine)),
            dma((n_fine,)), dma((n_coarse, n_fine)),
            dma((n_fine, n_coarse)), dma((n_fine, n_coarse)),
            dma((3,)), dma((3,)),
            dma((2, 2)), dma((2, 2)),
            dma((pairs,)), dma((pairs,)),
            dma, dma,
            dma((n_bits + n_coarse - 1, half)), dma((n_coarse, half)),
        ],
        compiler_params=pltpu.CompilerParams(
            collective_id=0, has_side_effects=True, vmem_limit_bytes=60 * 1024 * 1024
        ),
    )(*args)
    return encoded[None], decoded.reshape(1, count, width)


def solution(mesh):
    rows = P("doc", ("coarse", "fine"), None)
    placed = (rows,) * 7 + (P("doc", None, None), P("doc", None), P("doc", None))
    return jax.shard_map(
        local,
        mesh=mesh,
        in_specs=placed,
        out_specs=(rows, P("doc", None, None)),
        check_vma=False,
    )
```

time: 79.5 us -> 72.5 us (0.912); the launches traced: 78.5 us -> 72.3 us
  Pallas kernels: 73.9 us -> 67.8 us
    pallas_call x1, Pallas kernels: 73.9 us -> 67.8 us  [local(): pl.pallas_call(functools.partial(kernel, (n_coarse, n_fine, tokens, width...]
where the time goes in v1:
time: 72.5 us; the launch traced here: 72.3 us
  Pallas kernels  67.8 us (94%)
  local copies, waits for them, and re-layouts  3.93 us (5%)
    pallas_call x1, Pallas kernels, local(): pl.pallas_call(functools.partial(kernel, (n_coarse, n_fine, tokens, width...  67.8 us
    unnamed x2, local copies, waits for them, and re-layouts  3.93 us

profile of v1, /device:TPU:0, one launch (start us, length us, event | category | flops | bytes accessed | tf_op | source)
XLA Modules:
  0.0 72.3 jit_solution(11257212188873698167)
XLA Ops:
  0.6 67.8 %shard_map.95 = (bf16[128,1024]{1,0:T(8,128)(2,1)}, bf16[2,4,64,1024]{3,2,1,0:T(8,128)(2,1)}) custom-call(bf16[128,1024]{1,0:T(8,128)(2,1)} %bitcast.13, bf16[128,1024]{1,0:T(8,128)(2,1)} %bitcast.14, bf16[128,1024]{1,0:T(8,128)(2,1)} %bitcast.15, bf16[128,1024]{1,0:T(8,128)(2,1)} %bitcast.16, bf16[128,1024]{1,0:T(8,128)(2,1)} %bitcast.17, ...), custom_call_target="tpu_custom_call" | custom-call | tf_op jit(solution)/shard_map/pallas_call | solution.py:527
  68.4 1.7 %copy.12 = bf16[1,128,1024]{2,1,0:T(8,128)(2,1)} copy(bf16[1,128,1024]{2,1,0:T(8,128)(2,1)} %bitcast.12) | data formatting | bytes 524288
  70.1 2.3 %copy.13 = bf16[1,512,1024]{2,1,0:T(8,128)(2,1)} copy(bf16[1,512,1024]{2,1,0:T(8,128)(2,1)} %bitcast.10) | data formatting | bytes 2097152

commit v2 on v1

--- a/solution.py
+++ b/solution.py
@@ -263,24 +263,11 @@
 
     for d in range(1, n_q):
         enc_copy(d).start()
-    for d in range(1, pairs):
+    for d in [*range(pairs // 2, pairs), *range(1, pairs // 2)]:
         q_copy(d).start()
     loads[1].wait()
     loads[2].wait()
     kv_forward(0)
-    for d in range(1, n_fine):
-        for copy in kv_copy(d):
-            copy.start()
-    for copy in swap_copy():
-        copy.start()
-    loads[5].wait()
-    loads[6].wait()
-
-    for side in range(2):
-        @pl.when((lo == side) & has_peer[side])
-        def _():
-            for copy in halo_copy(side):
-                copy.start()
 
     row = lax.broadcasted_iota(jnp.int32, (tokens, 3 * tokens), 0)
     col = lax.broadcasted_iota(jnp.int32, (tokens, 3 * tokens), 1)
@@ -305,9 +292,23 @@
     enc_low().start()
     for d in range(1, n_coarse):
         enc_far(d, False).start()
+    for d in range(1, n_fine):
+        for copy in kv_copy(d):
+            copy.start()
+    loads[5].wait()
+    loads[6].wait()
+
+    for side in range(2):
+        @pl.when((lo == side) & has_peer[side])
+        def _():
+            for copy in halo_copy(side):
+                copy.start()
+
     enc_block(other).wait_recv()
     for d in range(1, n_coarse):
         enc_far(d, True).start()
+    for copy in swap_copy():
+        copy.start()
 
     for d in range(1, half):
         kv_forward(d)
@@ -512,6 +513,7 @@
     n_bits = half.bit_length() - 1
     mine = dec_queries.reshape(n_coarse, half, dec_rows, width)
     args = [q_light[0], k_light[0], v_light[0], q_heavy[0], k_heavy[0], v_heavy[0], enc_kv[0], mine]
+    args = [pltpu.with_memory_space_constraint(a, pltpu.HBM) for a in args]
     has_bias = key_ids.shape[1] != n_seq
     keys = n_coarse * half * tokens
     if has_bias:
@@ -565,7 +567,7 @@
             dma((n_bits + n_coarse - 1, half)), dma((n_coarse, half)),
         ],
         compiler_params=pltpu.CompilerParams(
-            collective_id=0, has_side_effects=True, vmem_limit_bytes=60 * 1024 * 1024
+            collective_id=0, has_side_effects=True, vmem_limit_bytes=32 * 1024 * 1024
         ),
     )(*args)
     return encoded[None], decoded.reshape(1, count, width)

time: 72.5 us -> 57.6 us (0.79)
  Pallas kernels: 67.8 us -> 55 us
  local copies, waits for them, and re-layouts: 3.93 us -> 1.67 us
    pallas_call x1, Pallas kernels: 67.8 us -> 55 us  [local(): pl.pallas_call(functools.partial(kernel, (n_coarse, n_fine, tokens, width...]
    unnamed x2, local copies, waits for them, and re-layouts: 3.93 us -> 1.67 us
where the time goes in v2:
time: 57.6 us; the launch traced here: 57.3 us
  Pallas kernels  55 us (95%)
  local copies, waits for them, and re-layouts  1.67 us (3%)
  between operations  0.64 us (1%)
    pallas_call x1, Pallas kernels, local(): pl.pallas_call(functools.partial(kernel, (n_coarse, n_fine, tokens, width...  55 us
    unnamed x2, local copies, waits for them, and re-layouts  1.67 us

profile of v2, /device:TPU:0, one launch (start us, length us, event | category | flops | bytes accessed | tf_op | source)
XLA Modules:
  0.0 57.3 jit_solution(18106935219052011009)
XLA Ops:
  0.6 55.0 %shard_map.95 = (bf16[128,1024]{1,0:T(8,128)(2,1)S(1)}, bf16[2,4,64,1024]{3,2,1,0:T(8,128)(2,1)S(1)}) custom-call(bf16[128,1024]{1,0:T(8,128)(2,1)} %bitcast.13, bf16[128,1024]{1,0:T(8,128)(2,1)} %bitcast.14, bf16[128,1024]{1,0:T(8,128)(2,1)} %bitcast.15, bf16[128,1024]{1,0:T(8,128)(2,1)} %bitcast.16, bf16[128,1024]{1,0:T(8,128)(2,1)} %bitcast.17, ...), custom_call_target="tpu_custom_call" | custom-call | tf_op jit(solution)/shard_map/pallas_call | solution.py:529
  55.7 0.7 %copy.12 = bf16[1,128,1024]{2,1,0:T(8,128)(2,1)} copy(bf16[1,128,1024]{2,1,0:T(8,128)(2,1)S(1)} %bitcast.11) | data formatting | bytes 524288
  56.4 1.0 %copy.13 = bf16[1,512,1024]{2,1,0:T(8,128)(2,1)} copy(bf16[1,512,1024]{2,1,0:T(8,128)(2,1)S(1)} %bitcast.10) | data formatting | bytes 2097152

commit v3 on v2

--- a/solution.py
+++ b/solution.py
@@ -57,9 +57,9 @@
     ql, kl, vl, qh, kh, vh, enc, decq = refs[:8]
     bias_ref = refs[8] if has_bias else None
     (out, dec, encbuf, drows, dq, do, qbuf, kbuf, vbuf, acc, stat, osend, orecv,
-     lq, lk, lv, lown, lsend, lrecv, band,
-     load_s, enc_s, enc_r, ek_s, ek_r, q_s, q_r, k_s, k_r, v_s, v_r, kx_s, vx_s,
-     x_s, x_r, h_s, h_r, o_s, o_r, lo_s, lo_r, dec_s, dec_r) = refs[8 + has_bias:]
+     lq, lk, lv, hop, lown, lsend, lrecv, band,
+     load_s, enc_s, enc_r, ey_s, ex_s, q_s, q_r, k_s, k_r, v_s, v_r, kx_s, vx_s,
+     far_s, x_s, x_r, h_s, h_r, hop_s, hop_r, o_s, o_r, lo_s, lo_r, dec_s, dec_r) = refs[8 + has_bias:]
 
     c = lax.axis_index("coarse")
     f = lax.axis_index("fine")
@@ -99,6 +99,15 @@
             body(d)
             return carry
         lax.fori_loop(start, stop, step, 0)
+
+    def begin(copies):
+        for copy in copies:
+            copy.start()
+
+    def begin_if(cond, copies):
+        @pl.when(cond)
+        def _():
+            begin(copies)
 
     loads = [
         pltpu.make_async_copy(enc, encbuf.at[me_kv, me_q], load_s.at[0]),
@@ -115,41 +124,86 @@
 
     barrier = pltpu.get_barrier_semaphore()
 
-    def greet(d, carry):
-        t = up(here, d, n_seq)
-        pl.semaphore_signal(
-            barrier, inc=1, device_id=at(lax.div(t, n_fine), lax.rem(t, n_fine)), device_id_type=MESH
-        )
-        return carry
-
-    lax.fori_loop(1, n_seq, greet, 0)
-    pl.semaphore_wait(barrier, n_seq - 1)
-
-    def at_q(a):
-        return at(c, a * LOW + lo)
-
-    def at_kv(b):
-        return at(lax.div(b, LOW), me_q * LOW + lax.rem(b, LOW))
-
-    def enc_copy(d):
-        return remote(enc, encbuf.at[me_kv, me_q], enc_s.at[d], enc_r.at[me_q], at_q(up(me_q, d, n_q)))
-
-    def enc_arrival(d):
-        src = down(me_q, d, n_q)
-        return remote(enc, encbuf.at[me_kv, src], enc_s.at[d], enc_r.at[src], at_q(src))
-
-    other = c * LOW + 1 - lo
-
-    def enc_low():
-        return remote(encbuf.at[me_kv], encbuf.at[me_kv], ek_s.at[0, 0], ek_r.at[me_kv], at_kv(other))
-
-    def enc_far(d, relay):
-        block = other if relay else me_kv
-        peer = up(c, d, n_coarse) * LOW + lo
-        return remote(encbuf.at[block], encbuf.at[block], ek_s.at[int(relay), d], ek_r.at[block], at_kv(peer))
-
-    def enc_block(block):
-        return remote(encbuf.at[block], encbuf.at[block], ek_s.at[0, 0], ek_r.at[block], at_kv(block))
+    has_up = me_q < n_q - 1
+    has_down = me_q > 0
+    n_near = n_coarse + has_up.astype(jnp.int32) + has_down.astype(jnp.int32)
+
+    def greet(sem):
+        def say(device):
+            pl.semaphore_signal(sem, inc=1, device_id=device, device_id_type=MESH)
+
+        say(at(c, f + 1 - 2 * lo))
+        for e in range(1, n_coarse):
+            say(at(up(c, e, n_coarse), f))
+
+        @pl.when(has_up)
+        def _():
+            say(at(c, jnp.minimum(f + LOW, n_fine - 1)))
+
+        @pl.when(has_down)
+        def _():
+            say(at(c, jnp.maximum(f - LOW, 0)))
+
+    greet(barrier)
+    pl.semaphore_wait(barrier, n_near)
+
+    def round_out(r):
+        greet(far_s.at[r])
+
+    def round_in(r):
+        pl.semaphore_wait(far_s.at[r], n_near)
+
+    def enc_row(way):
+        peer = jnp.clip(me_q + way, 0, n_q - 1)
+        return remote(
+            enc, encbuf.at[me_kv, me_q], enc_s.at[way + n_q - 1], enc_r.at[me_kv, me_q], at(c, peer * LOW + lo)
+        )
+
+    def enc_mate(block):
+        part = encbuf.at[me_kv, block]
+        return remote(part, part, ey_s.at[block], enc_r.at[me_kv, block], at(c, f + 1 - 2 * lo))
+
+    def enc_across(low, block, e):
+        part = encbuf.at[c * LOW + low, block]
+        return remote(
+            part, part, ex_s.at[low, e, block], enc_r.at[c * LOW + low, block], at(up(c, e, n_coarse), f)
+        )
+
+    def enc_wait(kv, block):
+        part = encbuf.at[kv, block]
+        remote(part, part, ey_s.at[block], enc_r.at[kv, block], at(c, f)).wait_recv()
+
+    def enc_out(block):
+        enc_mate(block).start()
+        for e in range(1, n_coarse):
+            enc_across(lo, block, e).start()
+
+    def enc_at(t):
+        for way in (t, -t):
+            row = me_q + way
+            yield way, jnp.clip(row, 0, n_q - 1), (row >= 0) & (row < n_q)
+
+    def enc_rows(t):
+        for way, row, there in enc_at(t):
+            begin_if(there, (enc_row(way),))
+
+    def enc_step(t):
+        for way, row, there in enc_at(t):
+            @pl.when(there)
+            def _():
+                enc_wait(me_kv, row)
+                enc_out(row)
+
+    def enc_turn(block):
+        enc_wait(c * LOW + 1 - lo, block)
+        for e in range(1, n_coarse):
+            enc_across(1 - lo, block, e).start()
+
+    def enc_side(t):
+        for way, row, there in enc_at(t):
+            @pl.when(there)
+            def _():
+                enc_turn(row)
 
     def q_copy(d):
         to = flip(p, d, pairs)
@@ -224,9 +278,44 @@
         )
 
     has_peer = [two > 0, two < n_pair_seq - 1]
-
-    def light_back():
-        return remote(lsend, lrecv, lo_s, lo_r, mate)
+    at_edge = [me_q == 0, me_q == n_q - 1]
+
+    def hop_copy(side):
+        peer = jnp.clip(c + 2 * side - 1, 0, n_coarse - 1)
+        return remote(lv.at[1 + side], hop, h_s.at[side, 1], hop_r, at(peer, f))
+
+    def hop_on(side):
+        end = (1 - side) * (n_q - 1)
+        slot = 3 - 3 * side
+        return remote(hop, lv.at[slot], hop_s, h_r.at[side, 1], at(c, end * LOW + lo))
+
+    hops_here = [at_edge[0] & (c < n_coarse - 1), at_edge[1] & (c > 0)]
+
+    def halo_send(side, mine):
+        go = mine & has_peer[side]
+        keys, values = halo_copy(side)
+
+        @pl.when(go)
+        def _():
+            keys.start()
+
+        @pl.when(go & jnp.logical_not(at_edge[side]))
+        def _():
+            values.start()
+
+        @pl.when(go & at_edge[side])
+        def _():
+            hop_copy(side).start()
+
+    def hop_forward():
+        for side in range(2):
+            @pl.when(hops_here[side])
+            def _():
+                hop_copy(side).wait_recv()
+                hop_on(side).start()
+
+    def light_back(j):
+        return remote(lsend.at[j], lrecv.at[j], lo_s.at[j], lo_r.at[j], mate)
 
     bits = []
     bit = half // 2
@@ -247,28 +336,45 @@
         return remote(part, part, dec_s.at[0, 0], dec_r.at[cc, block], at(cc, f))
 
     def dec_spread(block, first):
-        for k in range(first, len(bits) + n_coarse - 1):
+        for k in range(first, len(bits)):
             dec_copy(block, k).start()
 
-    def dec_stage(k):
-        done = [0]
-        for b in bits[:k]:
-            done = done + [x + b for x in done]
-        return [flip(g, x + bits[k], half) for x in done]
-
-    def dec_forward(k):
-        for block in dec_stage(k):
-            dec_arrival(c, block).wait_recv()
-            dec_spread(block, k + 1)
-
-    for d in range(1, n_q):
-        enc_copy(d).start()
-    for d in [*range(pairs // 2, pairs), *range(1, pairs // 2)]:
-        q_copy(d).start()
+    def dec_across(block):
+        for k in range(len(bits), len(bits) + n_coarse - 1):
+            dec_copy(block, k).start()
+
+    def dec_wave(steps):
+        for x in range(1, half):
+            if bin(x).count("1") == steps:
+                block = flip(g, x, half)
+                last = bits.index(x & -x)
+                dec_arrival(c, block).wait_recv()
+                dec_spread(block, last + 1)
+                dec_across(block)
+
+    def q_of(d):
+        return (q_copy(d // share),) if d % share == 0 else ()
+
+    def rows_next(d):
+        return jnp.abs(lax.div(flip(f, d, n_fine), LOW) - me_q) == 1
+
+    even_near, even_far = range(2, half, 2), range(half, n_fine, 2)
+    odd_near, odd_far = range(3, half, 2), range(half + 1, n_fine, 2)
+    even = [*even_near, *even_far]
+
+    round_out(1)
+    enc_rows(1)
+    loads[0].wait()
+    enc_out(me_q)
+    for d in even:
+        begin_if(rows_next(d), q_of(d))
+    begin(q_of(1))
     loads[1].wait()
     loads[2].wait()
     kv_forward(0)
-
+    for d in even:
+        begin_if(rows_next(d), kv_copy(d))
+    begin(kv_copy(1))
     row = lax.broadcasted_iota(jnp.int32, (tokens, 3 * tokens), 0)
     col = lax.broadcasted_iota(jnp.int32, (tokens, 3 * tokens), 1)
     for b in range(LOW):
@@ -286,37 +392,34 @@
         )
         dq[2 * j * dec_rows:(2 * j + 2) * dec_rows, :] = both.astype(jnp.bfloat16)
 
-    loads[0].wait()
-    for d in range(1, n_q):
-        enc_arrival(d).wait_recv()
-    enc_low().start()
-    for d in range(1, n_coarse):
-        enc_far(d, False).start()
-    for d in range(1, n_fine):
-        for copy in kv_copy(d):
-            copy.start()
-    loads[5].wait()
-    loads[6].wait()
-
-    for side in range(2):
-        @pl.when((lo == side) & has_peer[side])
-        def _():
-            for copy in halo_copy(side):
-                copy.start()
-
-    enc_block(other).wait_recv()
-    for d in range(1, n_coarse):
-        enc_far(d, True).start()
-    for copy in swap_copy():
-        copy.start()
-
-    for d in range(1, half):
+    for r in range(1, n_q - 1):
+        round_in(r)
+        round_out(r + 1)
+    enc_step(1)
+    round_in(n_q - 1)
+    for t in range(2, n_q):
+        enc_rows(t)
+    for d in [*odd_near, *even]:
+        begin_if(jnp.logical_not(rows_next(d)) if d % 2 == 0 else here >= 0, q_of(d))
+    for d in odd_far:
+        begin(q_of(d))
+    for d in odd_near:
+        begin(kv_copy(d))
+    enc_turn(me_q)
+    enc_side(1)
+    for d in even:
+        begin_if(jnp.logical_not(rows_next(d)), kv_copy(d))
+    for d in range(2, half, 2):
         kv_forward(d)
-
-    for d in range(1, n_coarse):
-        for part in range(LOW):
-            enc_block(up(c, d, n_coarse) * LOW + part).wait_recv()
-
+    for d in range(1, half, 2):
+        kv_forward(d)
+    for t in range(2, n_q):
+        enc_step(t)
+    for d in odd_far:
+        begin(kv_copy(d))
+    begin(swap_copy())
+    far = [*range(half, n_fine, 2), *range(half + 1, n_fine, 2)]
+    quarter = len(far) // 4
     d_total = heads * dec_rows
     d_chunk = min(256, d_total)
 
@@ -328,15 +431,6 @@
         total = jnp.sum(e, axis=1, keepdims=True)
         do[rows, :] = dot(e.astype(jnp.bfloat16), kv) / total
 
-    loop(0, d_total // d_chunk, dec_step)
-    for j in range(pairs):
-        even = do[2 * j * dec_rows:(2 * j + 1) * dec_rows, :]
-        odd = do[(2 * j + 1) * dec_rows:(2 * j + 2) * dec_rows, :]
-        dec[c, g, :, j * PAIR:(j + 1) * PAIR] = jnp.where(
-            lane_d < HEAD, pltpu.roll(even, HEAD, 1), odd
-        ).astype(jnp.bfloat16)
-    dec_spread(g, 0)
-
     low_half = lax.broadcasted_iota(jnp.int32, (tokens, PAIR), 1) < HEAD
     lane_2 = lax.broadcasted_iota(jnp.int32, (2 * tokens, PAIR), 1)
     keys = n_coarse * half * tokens
@@ -351,7 +445,8 @@
     def heavy_values(part):
         return vbuf[:, pl.ds(part * half, half)].reshape(keys, PAIR)
 
-    def heavy_first(j):
+    def heavy_first(d):
+        j = flip(p, d, pairs)
         s = heavy_scores(j, hh)
         peak = jnp.max(s, axis=1, keepdims=True)
         e = jnp.exp(s - peak)
@@ -370,31 +465,54 @@
         return jnp.where(low_half, o[:tokens], o[tokens:]).astype(jnp.bfloat16)
 
     loads[3].wait()
-    for d in range(1, pairs):
+    for d in range(1, pairs // 2):
         q_arrival(d).wait_recv()
     for e in range(1, n_coarse):
         for i in range(half):
             for copy in kv_block(up(c, e, n_coarse), hh * half + i):
                 copy.wait_recv()
-    per = max(1, pairs // half)
-    done = 0
-    for r in range(half):
-        stop = pairs if r == half - 1 else min(pairs, done + per)
-        loop(done, stop, heavy_first)
-        done = stop
-        kv_forward(half + r)
-
-    for k in range(len(bits) - 1):
-        dec_forward(k)
+    loop(0, pairs // 2, heavy_first)
+    for t in range(2, n_q):
+        enc_side(t)
     arrived = swap_arrival()
+    n_chunk = d_total // d_chunk
+    for d in range(pairs // 2, pairs):
+        q_arrival(d).wait_recv()
+    loop(pairs // 2, pairs, heavy_first)
+    for d in far[0 * quarter:1 * quarter]:
+        kv_forward(d)
+    for d in range(1, n_coarse):
+        for part in range(LOW):
+            for block in range(n_q):
+                enc_wait(up(c, d, n_coarse) * LOW + part, block)
+
+    loop(0 * n_chunk // 4, 1 * n_chunk // 4, dec_step)
+    for d in far[1 * quarter:2 * quarter]:
+        kv_forward(d)
+    loop(1 * n_chunk // 4, 2 * n_chunk // 4, dec_step)
+    for d in far[2 * quarter:3 * quarter]:
+        kv_forward(d)
+    loads[5].wait()
+    loads[6].wait()
+    for side in range(2):
+        halo_send(side, lo == side)
+    loop(2 * n_chunk // 4, 3 * n_chunk // 4, dec_step)
+    for d in far[3 * quarter:4 * quarter]:
+        kv_forward(d)
+    loop(3 * n_chunk // 4, n_chunk, dec_step)
+    for j in range(pairs):
+        even = do[2 * j * dec_rows:(2 * j + 1) * dec_rows, :]
+        odd = do[(2 * j + 1) * dec_rows:(2 * j + 2) * dec_rows, :]
+        dec[c, g, :, j * PAIR:(j + 1) * PAIR] = jnp.where(
+            lane_d < HEAD, pltpu.roll(even, HEAD, 1), odd
+        ).astype(jnp.bfloat16)
+    dec_spread(g, 0)
     arrived[0].wait_recv()
     arrived[1].wait_recv()
     for side in range(2):
-        @pl.when((lo == 1 - side) & has_peer[side])
-        def _():
-            for copy in halo_copy(side):
-                copy.start()
-
+        halo_send(side, lo == 1 - side)
+    hop_forward()
+    dec_across(g)
     for e in range(1, n_coarse):
         for i in range(half):
             for copy in kv_block(up(c, e, n_coarse), (1 - hh) * half + i):
@@ -406,9 +524,10 @@
         osend[j] = heavy_second(j)
         o_copy(d).start()
 
-    loop(0, pairs - 1, heavy_out)
+    loop(0, pairs // 2, heavy_out)
+    dec_wave(1)
+    loop(pairs // 2, pairs - 1, heavy_out)
     orecv[p] = heavy_second(p)
-    dec_forward(len(bits) - 1)
 
     arrived[2].wait_recv()
     loads[7].wait()
@@ -435,13 +554,15 @@
         return jnp.where(low_half, o[:tokens], o[tokens:])
 
     def light_away(j):
-        lsend[:, cols_of(j)] = light_of(1 - lo, j).astype(jnp.bfloat16)
+        lsend[j] = light_of(1 - lo, j).astype(jnp.bfloat16)
+        light_back(j).start()
 
     def light_home(j):
         lown[:, cols_of(j)] = light_of(lo, j)
 
     loop(0, pairs_half, light_away)
-    light_back().start()
+    for steps in range(2, len(bits) + 1):
+        dec_wave(steps)
     loop(0, pairs_half, light_home)
 
     for d in range(1, pairs):
@@ -455,21 +576,27 @@
     def join_away(j):
         pair = (1 - lo) * pairs_half + j
         heavy = orecv[pair].astype(jnp.float32)
-        out[:, cols_of(pair)] = (lrecv[:, cols_of(j)].astype(jnp.float32) + heavy).astype(jnp.bfloat16)
+        out[:, cols_of(pair)] = (lrecv[j].astype(jnp.float32) + heavy).astype(jnp.bfloat16)
 
     loop(0, pairs_half, join_home)
-    light_back().wait_recv()
+    for j in range(pairs_half):
+        light_back(j).wait_recv()
     loop(0, pairs_half, join_away)
 
     for e in range(1, n_coarse):
         for block in range(half):
             dec_arrival(up(c, e, n_coarse), block).wait_recv()
-    for d in range(1, n_q):
-        enc_copy(d).wait_send()
-    enc_low().wait_send()
-    for d in range(1, n_coarse):
-        enc_far(d, False).wait_send()
-        enc_far(d, True).wait_send()
+    for t in range(1, n_q):
+        for way, row, there in enc_at(t):
+            @pl.when(there)
+            def _():
+                enc_row(way).wait_send()
+
+    for block in range(n_q):
+        enc_mate(block).wait_send()
+        for low in range(LOW):
+            for e in range(1, n_coarse):
+                enc_across(low, block, e).wait_send()
     for d in range(1, pairs):
         q_copy(d).wait_send()
         o_copy(d).wait_send()
@@ -482,12 +609,17 @@
                 copy.wait_send()
     for copy in swap_copy():
         copy.wait_send()
-    light_back().wait_send()
+    for j in range(pairs_half):
+        light_back(j).wait_send()
     for side in range(2):
         @pl.when(has_peer[side])
         def _():
             for copy in halo_copy(side):
                 copy.wait_send()
+
+        @pl.when(hops_here[side])
+        def _():
+            hop_on(side).wait_send()
     for k in range(len(bits) + n_coarse - 1):
         sent = [0]
         for b in bits[:k]:
@@ -549,21 +681,24 @@
             pltpu.VMEM((2, tokens, wide), bf16),
             pltpu.VMEM((4, tokens, wide), bf16),
             pltpu.VMEM((4, tokens, wide), bf16),
+            pltpu.VMEM((tokens, wide), bf16),
             pltpu.VMEM((tokens, wide), f32),
-            pltpu.VMEM((tokens, wide), bf16),
-            pltpu.VMEM((tokens, wide), bf16),
+            pltpu.VMEM((pairs // LOW, tokens, PAIR), bf16),
+            pltpu.VMEM((pairs // LOW, tokens, PAIR), bf16),
             pltpu.VMEM((2, tokens, 3 * tokens), f32),
             dma((8,)),
-            dma((n_q,)), dma((n_q,)),
-            dma((2, n_coarse)), dma((n_kv,)),
+            dma((2 * n_q - 1,)), dma((n_kv, n_q)),
+            dma((n_q,)), dma((LOW, n_coarse, n_q)),
             dma((pairs,)), dma((pairs,)),
             dma((n_fine,)), dma((n_coarse, n_fine)),
             dma((n_fine,)), dma((n_coarse, n_fine)),
             dma((n_fine, n_coarse)), dma((n_fine, n_coarse)),
+            pltpu.SemaphoreType.REGULAR((n_q,)),
             dma((3,)), dma((3,)),
             dma((2, 2)), dma((2, 2)),
+            dma, dma,
             dma((pairs,)), dma((pairs,)),
-            dma, dma,
+            dma((pairs // LOW,)), dma((pairs // LOW,)),
             dma((n_bits + n_coarse - 1, half)), dma((n_coarse, half)),
         ],
         compiler_params=pltpu.CompilerParams(

time: 57.6 us -> 52.7 us (0.915)
  Pallas kernels: 55 us -> 50.2 us
    pallas_call x1, Pallas kernels: 55 us -> 50.2 us  [local(): pl.pallas_call(functools.partial(kernel, (n_coarse, n_fine, tokens, width...]
where the time goes in v3:
time: 52.7 us; the launch traced here: 52.5 us
  Pallas kernels  50.2 us (95%)
  local copies, waits for them, and re-layouts  1.67 us (3%)
  between operations  0.64 us (1%)
    pallas_call x1, Pallas kernels, local(): pl.pallas_call(functools.partial(kernel, (n_coarse, n_fine, tokens, width...  50.2 us
    unnamed x2, local copies, waits for them, and re-layouts  1.67 us

profile of v3, /device:TPU:0, one launch (start us, length us, event | category | flops | bytes accessed | tf_op | source)
XLA Modules:
  0.0 52.5 jit_solution(7576708828871120916)
XLA Ops:
  0.6 50.2 %shard_map.95 = (bf16[128,1024]{1,0:T(8,128)(2,1)S(1)}, bf16[2,4,64,1024]{3,2,1,0:T(8,128)(2,1)S(1)}) custom-call(bf16[128,1024]{1,0:T(8,128)(2,1)} %bitcast.13, bf16[128,1024]{1,0:T(8,128)(2,1)} %bitcast.14, bf16[128,1024]{1,0:T(8,128)(2,1)} %bitcast.15, bf16[128,1024]{1,0:T(8,128)(2,1)} %bitcast.16, bf16[128,1024]{1,0:T(8,128)(2,1)} %bitcast.17, ...), custom_call_target="tpu_custom_call" | custom-call | tf_op jit(solution)/shard_map/pallas_call | solution.py:661
  50.9 0.7 %copy.12 = bf16[1,128,1024]{2,1,0:T(8,128)(2,1)} copy(bf16[1,128,1024]{2,1,0:T(8,128)(2,1)S(1)} %bitcast.11) | data formatting | bytes 524288
  51.6 1.0 %copy.13 = bf16[1,512,1024]{2,1,0:T(8,128)(2,1)} copy(bf16[1,512,1024]{2,1,0:T(8,128)(2,1)S(1)} %bitcast.10) | data formatting | bytes 2097152

commit v4 on v3

--- a/solution.py
+++ b/solution.py
@@ -56,9 +56,9 @@
     refs = list(refs)
     ql, kl, vl, qh, kh, vh, enc, decq = refs[:8]
     bias_ref = refs[8] if has_bias else None
-    (out, dec, encbuf, drows, dq, do, qbuf, kbuf, vbuf, acc, stat, osend, orecv,
+    (out, dec, encbuf, drows, dq, do, qbuf, kvbuf, acc, stat, osend, orecv,
      lq, lk, lv, hop, lown, lsend, lrecv, band,
-     load_s, enc_s, enc_r, ey_s, ex_s, q_s, q_r, k_s, k_r, v_s, v_r, kx_s, vx_s,
+     load_s, enc_s, enc_r, ey_s, ex_s, q_s, q_r, kv_s, kv_r, kx_s,
      far_s, x_s, x_r, h_s, h_r, hop_s, hop_r, o_s, o_r, lo_s, lo_r, dec_s, dec_r) = refs[8 + has_bias:]
 
     c = lax.axis_index("coarse")
@@ -79,6 +79,12 @@
             device_id=device, device_id_type=MESH,
         )
 
+    def take(ref, sem):
+        remote(ref, ref, sem, sem, at(c, f)).wait_recv()
+
+    def drain(ref, sem):
+        remote(ref, ref, sem, sem, at(c, f)).wait_send()
+
     def up(me, d, n):
         return lax.rem(me + d, n)
 
@@ -111,13 +117,13 @@
 
     loads = [
         pltpu.make_async_copy(enc, encbuf.at[me_kv, me_q], load_s.at[0]),
-        pltpu.make_async_copy(kh.at[:, cols_of(p)], kbuf.at[c, f], load_s.at[1]),
-        pltpu.make_async_copy(vh.at[:, cols_of(p)], vbuf.at[c, f], load_s.at[2]),
-        pltpu.make_async_copy(qh.at[:, cols_of(p)], qbuf.at[p], load_s.at[3]),
-        pltpu.make_async_copy(decq.at[c, g], drows, load_s.at[4]),
-        pltpu.make_async_copy(kl.at[:, side_of(lo)], lk.at[1 + lo], load_s.at[5]),
-        pltpu.make_async_copy(vl.at[:, side_of(lo)], lv.at[1 + lo], load_s.at[6]),
-        pltpu.make_async_copy(ql.at[:, side_of(lo)], lq.at[lo], load_s.at[7]),
+        pltpu.make_async_copy(kh.at[:, cols_of(p)], kvbuf.at[c, f, 0], load_s.at[1]),
+        pltpu.make_async_copy(vh.at[:, cols_of(p)], kvbuf.at[c, f, 1], load_s.at[1]),
+        pltpu.make_async_copy(qh.at[:, cols_of(p)], qbuf.at[p], load_s.at[2]),
+        pltpu.make_async_copy(decq.at[c, g], drows, load_s.at[3]),
+        pltpu.make_async_copy(kl.at[:, side_of(lo)], lk.at[1 + lo], load_s.at[4]),
+        pltpu.make_async_copy(vl.at[:, side_of(lo)], lv.at[1 + lo], load_s.at[4]),
+        pltpu.make_async_copy(ql.at[:, side_of(lo)], lq.at[lo], load_s.at[5]),
     ]
     for copy in loads:
         copy.start()
@@ -156,22 +162,16 @@
     def enc_row(way):
         peer = jnp.clip(me_q + way, 0, n_q - 1)
         return remote(
-            enc, encbuf.at[me_kv, me_q], enc_s.at[way + n_q - 1], enc_r.at[me_kv, me_q], at(c, peer * LOW + lo)
+            enc, encbuf.at[me_kv, me_q], enc_s, enc_r.at[me_q], at(c, peer * LOW + lo)
         )
 
     def enc_mate(block):
         part = encbuf.at[me_kv, block]
-        return remote(part, part, ey_s.at[block], enc_r.at[me_kv, block], at(c, f + 1 - 2 * lo))
+        return remote(part, part, ey_s, enc_r.at[n_q + block], at(c, f + 1 - 2 * lo))
 
     def enc_across(low, block, e):
         part = encbuf.at[c * LOW + low, block]
-        return remote(
-            part, part, ex_s.at[low, e, block], enc_r.at[c * LOW + low, block], at(up(c, e, n_coarse), f)
-        )
-
-    def enc_wait(kv, block):
-        part = encbuf.at[kv, block]
-        remote(part, part, ey_s.at[block], enc_r.at[kv, block], at(c, f)).wait_recv()
+        return remote(part, part, ex_s, enc_r.at[2 * n_q], at(up(c, e, n_coarse), f))
 
     def enc_out(block):
         enc_mate(block).start()
@@ -191,11 +191,11 @@
         for way, row, there in enc_at(t):
             @pl.when(there)
             def _():
-                enc_wait(me_kv, row)
+                take(encbuf.at[me_kv, row], enc_r.at[row])
                 enc_out(row)
 
     def enc_turn(block):
-        enc_wait(c * LOW + 1 - lo, block)
+        take(encbuf.at[c * LOW + 1 - lo, block], enc_r.at[n_q + block])
         for e in range(1, n_coarse):
             enc_across(1 - lo, block, e).start()
 
@@ -207,65 +207,39 @@
 
     def q_copy(d):
         to = flip(p, d, pairs)
-        return remote(qh.at[:, cols_of(to)], qbuf.at[p], q_s.at[d], q_r.at[p], at(c, to * share + s_me))
-
-    def q_arrival(d):
-        src = flip(p, d, pairs)
-        return remote(qbuf.at[src], qbuf.at[src], q_s.at[d], q_r.at[src], at(c, src * share + s_me))
+        return remote(qh.at[:, cols_of(to)], qbuf.at[p], q_s, q_r.at[int(d >= pairs // 2)], at(c, to * share + s_me))
 
     def kv_copy(d):
         to = flip(f, d, n_fine)
         col = cols_of(lax.div(to, share))
         return (
-            remote(kh.at[:, col], kbuf.at[c, f], k_s.at[d], k_r.at[c, f], at(c, to)),
-            remote(vh.at[:, col], vbuf.at[c, f], v_s.at[d], v_r.at[c, f], at(c, to)),
+            remote(kh.at[:, col], kvbuf.at[c, f, 0], kv_s, kv_r.at[f], at(c, to)),
+            remote(vh.at[:, col], kvbuf.at[c, f, 1], kv_s, kv_r.at[f], at(c, to)),
         )
 
-    def kv_block(cc, ff):
-        return (
-            remote(kbuf.at[cc, ff], kbuf.at[cc, ff], k_s.at[0], k_r.at[cc, ff], at(cc, ff)),
-            remote(vbuf.at[cc, ff], vbuf.at[cc, ff], v_s.at[0], v_r.at[cc, ff], at(cc, ff)),
-        )
-
-    def kv_relay(d, e):
+    def kv_forward(d):
         src = flip(f, d, n_fine)
-        peer = at(up(c, e, n_coarse), f)
-        return (
-            remote(kbuf.at[c, src], kbuf.at[c, src], kx_s.at[d, e], k_r.at[c, src], peer),
-            remote(vbuf.at[c, src], vbuf.at[c, src], vx_s.at[d, e], v_r.at[c, src], peer),
-        )
-
-    def kv_forward(d):
+        block = kvbuf.at[c, src]
         if d:
-            for copy in kv_block(c, flip(f, d, n_fine)):
-                copy.wait_recv()
+            take(block, kv_r.at[src])
         for e in range(1, n_coarse):
-            for copy in kv_relay(d, e):
-                copy.start()
+            remote(block, block, kx_s, kv_r.at[n_fine + int(d >= half)], at(up(c, e, n_coarse), f)).start()
+
+    def kv_others(far_half):
+        take(kvbuf.at[pl.ds(0, n_coarse - 1), pl.ds(0, half)], kv_r.at[n_fine + far_half])
 
     def o_copy(d):
         to = flip(p, d, pairs)
-        return remote(osend.at[to], orecv.at[p], o_s.at[d], o_r.at[p], at(c, to * share + s_me))
-
-    def o_arrival(d):
-        src = flip(p, d, pairs)
-        return remote(osend.at[src], orecv.at[src], o_s.at[d], o_r.at[src], at(c, src * share + s_me))
+        return remote(osend.at[to], orecv.at[p], o_s, o_r, at(c, to * share + s_me))
 
     mate = at(c, f + 1 - 2 * lo)
 
     def swap_copy():
         cols = side_of(1 - lo)
         return (
-            remote(kl.at[:, cols], lk.at[1 + lo], x_s.at[0], x_r.at[0], mate),
-            remote(vl.at[:, cols], lv.at[1 + lo], x_s.at[1], x_r.at[1], mate),
-            remote(ql.at[:, cols], lq.at[lo], x_s.at[2], x_r.at[2], mate),
-        )
-
-    def swap_arrival():
-        return (
-            remote(lk.at[2 - lo], lk.at[2 - lo], x_s.at[0], x_r.at[0], mate),
-            remote(lv.at[2 - lo], lv.at[2 - lo], x_s.at[1], x_r.at[1], mate),
-            remote(lq.at[1 - lo], lq.at[1 - lo], x_s.at[2], x_r.at[2], mate),
+            remote(kl.at[:, cols], lk.at[1 + lo], x_s, x_r.at[0], mate),
+            remote(vl.at[:, cols], lv.at[1 + lo], x_s, x_r.at[0], mate),
+            remote(ql.at[:, cols], lq.at[lo], x_s, x_r.at[1], mate),
         )
 
     def halo_copy(side):
@@ -273,8 +247,8 @@
         device = at(lax.div(peer, n_fine), lax.rem(peer, n_fine))
         slot = 3 - 3 * side
         return (
-            remote(lk.at[1 + side], lk.at[slot], h_s.at[side, 0], h_r.at[side, 0], device),
-            remote(lv.at[1 + side], lv.at[slot], h_s.at[side, 1], h_r.at[side, 1], device),
+            remote(lk.at[1 + side], lk.at[slot], h_s.at[side], h_r.at[side], device),
+            remote(lv.at[1 + side], lv.at[slot], h_s.at[side], h_r.at[side], device),
         )
 
     has_peer = [two > 0, two < n_pair_seq - 1]
@@ -282,12 +256,12 @@
 
     def hop_copy(side):
         peer = jnp.clip(c + 2 * side - 1, 0, n_coarse - 1)
-        return remote(lv.at[1 + side], hop, h_s.at[side, 1], hop_r, at(peer, f))
+        return remote(lv.at[1 + side], hop, h_s.at[side], hop_r, at(peer, f))
 
     def hop_on(side):
         end = (1 - side) * (n_q - 1)
         slot = 3 - 3 * side
-        return remote(hop, lv.at[slot], hop_s, h_r.at[side, 1], at(c, end * LOW + lo))
+        return remote(hop, lv.at[slot], hop_s, h_r.at[side], at(c, end * LOW + lo))
 
     hops_here = [at_edge[0] & (c < n_coarse - 1), at_edge[1] & (c > 0)]
 
@@ -315,7 +289,7 @@
                 hop_on(side).start()
 
     def light_back(j):
-        return remote(lsend.at[j], lrecv.at[j], lo_s.at[j], lo_r.at[j], mate)
+        return remote(lsend.at[j], lrecv.at[j], lo_s, lo_r, mate)
 
     bits = []
     bit = half // 2
@@ -329,11 +303,7 @@
             peer = at(c, hh * half + flip(g, bits[k], half))
         else:
             peer = at(up(c, k - len(bits) + 1, n_coarse), f)
-        return remote(mine, mine, dec_s.at[k, block], dec_r.at[c, block], peer)
-
-    def dec_arrival(cc, block):
-        part = dec.at[cc, block]
-        return remote(part, part, dec_s.at[0, 0], dec_r.at[cc, block], at(cc, f))
+        return remote(mine, mine, dec_s.at[k], dec_r.at[block if k < len(bits) else half], peer)
 
     def dec_spread(block, first):
         for k in range(first, len(bits)):
@@ -348,7 +318,7 @@
             if bin(x).count("1") == steps:
                 block = flip(g, x, half)
                 last = bits.index(x & -x)
-                dec_arrival(c, block).wait_recv()
+                take(dec.at[c, block], dec_r.at[block])
                 dec_spread(block, last + 1)
                 dec_across(block)
 
@@ -369,8 +339,7 @@
     for d in even:
         begin_if(rows_next(d), q_of(d))
     begin(q_of(1))
-    loads[1].wait()
-    loads[2].wait()
+    pltpu.make_async_copy(kvbuf.at[c, f], kvbuf.at[c, f], load_s.at[1]).wait()
     kv_forward(0)
     for d in even:
         begin_if(rows_next(d), kv_copy(d))
@@ -437,13 +406,13 @@
 
     def heavy_scores(j, part):
         q = stacked_pair(qbuf[j], low_half)
-        s = dot_t(q, kbuf[:, pl.ds(part * half, half)].reshape(keys, PAIR))
+        s = dot_t(q, kvbuf[:, pl.ds(part * half, half), 0].reshape(keys, PAIR))
         if has_bias:
             s = s + bias_ref[part, 0:1, :]
         return s
 
     def heavy_values(part):
-        return vbuf[:, pl.ds(part * half, half)].reshape(keys, PAIR)
+        return kvbuf[:, pl.ds(part * half, half), 1].reshape(keys, PAIR)
 
     def heavy_first(d):
         j = flip(p, d, pairs)
@@ -465,26 +434,17 @@
         return jnp.where(low_half, o[:tokens], o[tokens:]).astype(jnp.bfloat16)
 
     loads[3].wait()
-    for d in range(1, pairs // 2):
-        q_arrival(d).wait_recv()
-    for e in range(1, n_coarse):
-        for i in range(half):
-            for copy in kv_block(up(c, e, n_coarse), hh * half + i):
-                copy.wait_recv()
+    take(qbuf.at[pl.ds(0, pairs // 2 - 1)], q_r.at[0])
+    kv_others(0)
     loop(0, pairs // 2, heavy_first)
     for t in range(2, n_q):
         enc_side(t)
-    arrived = swap_arrival()
     n_chunk = d_total // d_chunk
-    for d in range(pairs // 2, pairs):
-        q_arrival(d).wait_recv()
+    take(qbuf.at[pl.ds(0, pairs // 2)], q_r.at[1])
     loop(pairs // 2, pairs, heavy_first)
     for d in far[0 * quarter:1 * quarter]:
         kv_forward(d)
-    for d in range(1, n_coarse):
-        for part in range(LOW):
-            for block in range(n_q):
-                enc_wait(up(c, d, n_coarse) * LOW + part, block)
+    take(encbuf.at[pl.ds(0, LOW * (n_coarse - 1))], enc_r.at[2 * n_q])
 
     loop(0 * n_chunk // 4, 1 * n_chunk // 4, dec_step)
     for d in far[1 * quarter:2 * quarter]:
@@ -492,8 +452,7 @@
     loop(1 * n_chunk // 4, 2 * n_chunk // 4, dec_step)
     for d in far[2 * quarter:3 * quarter]:
         kv_forward(d)
-    loads[5].wait()
-    loads[6].wait()
+    pltpu.make_async_copy(lk.at[pl.ds(0, 2)], lk.at[pl.ds(0, 2)], load_s.at[4]).wait()
     for side in range(2):
         halo_send(side, lo == side)
     loop(2 * n_chunk // 4, 3 * n_chunk // 4, dec_step)
@@ -507,16 +466,12 @@
             lane_d < HEAD, pltpu.roll(even, HEAD, 1), odd
         ).astype(jnp.bfloat16)
     dec_spread(g, 0)
-    arrived[0].wait_recv()
-    arrived[1].wait_recv()
+    take(lk.at[pl.ds(0, 2)], x_r.at[0])
     for side in range(2):
         halo_send(side, lo == 1 - side)
     hop_forward()
     dec_across(g)
-    for e in range(1, n_coarse):
-        for i in range(half):
-            for copy in kv_block(up(c, e, n_coarse), (1 - hh) * half + i):
-                copy.wait_recv()
+    kv_others(1)
 
     def heavy_out(i):
         d = pairs - 1 - i
@@ -529,13 +484,12 @@
     loop(pairs // 2, pairs - 1, heavy_out)
     orecv[p] = heavy_second(p)
 
-    arrived[2].wait_recv()
+    take(lq.at[1 - lo], x_r.at[1])
     loads[7].wait()
     for side in range(2):
         @pl.when(has_peer[side])
         def _():
-            for copy in halo_copy(1 - side):
-                copy.wait_recv()
+            take(lk.at[pl.ds(0, 2)], h_r.at[1 - side])
 
         @pl.when(jnp.logical_not(has_peer[side]))
         def _():
@@ -565,8 +519,7 @@
         dec_wave(steps)
     loop(0, pairs_half, light_home)
 
-    for d in range(1, pairs):
-        o_arrival(d).wait_recv()
+    take(orecv.at[pl.ds(0, pairs - 1)], o_r)
 
     def join_home(j):
         pair = lo * pairs_half + j
@@ -579,53 +532,29 @@
         out[:, cols_of(pair)] = (lrecv[j].astype(jnp.float32) + heavy).astype(jnp.bfloat16)
 
     loop(0, pairs_half, join_home)
-    for j in range(pairs_half):
-        light_back(j).wait_recv()
+    take(lrecv, lo_r)
     loop(0, pairs_half, join_away)
 
-    for e in range(1, n_coarse):
-        for block in range(half):
-            dec_arrival(up(c, e, n_coarse), block).wait_recv()
-    for t in range(1, n_q):
-        for way, row, there in enc_at(t):
-            @pl.when(there)
-            def _():
-                enc_row(way).wait_send()
-
-    for block in range(n_q):
-        enc_mate(block).wait_send()
-        for low in range(LOW):
-            for e in range(1, n_coarse):
-                enc_across(low, block, e).wait_send()
-    for d in range(1, pairs):
-        q_copy(d).wait_send()
-        o_copy(d).wait_send()
-    for d in range(n_fine):
-        if d:
-            for copy in kv_copy(d):
-                copy.wait_send()
-        for e in range(1, n_coarse):
-            for copy in kv_relay(d, e):
-                copy.wait_send()
-    for copy in swap_copy():
-        copy.wait_send()
-    for j in range(pairs_half):
-        light_back(j).wait_send()
+    take(dec.at[pl.ds(0, n_coarse - 1)], dec_r.at[half])
+    drain(encbuf.at[0, pl.ds(0, n_q - 1)], enc_s)
+    drain(encbuf.at[0], ey_s)
+    drain(encbuf.at[pl.ds(0, LOW * (n_coarse - 1))], ex_s)
+    drain(qbuf.at[pl.ds(0, pairs - 1)], q_s)
+    drain(osend.at[pl.ds(0, pairs - 1)], o_s)
+    drain(kvbuf.at[0, pl.ds(0, n_fine - 1)], kv_s)
+    drain(kvbuf.at[pl.ds(0, n_coarse - 1)], kx_s)
+    drain(lk.at[pl.ds(0, 3)], x_s)
+    drain(lsend, lo_s)
     for side in range(2):
         @pl.when(has_peer[side])
         def _():
-            for copy in halo_copy(side):
-                copy.wait_send()
+            drain(lk.at[pl.ds(0, 2)], h_s.at[side])
 
         @pl.when(hops_here[side])
         def _():
-            hop_on(side).wait_send()
+            drain(hop, hop_s)
     for k in range(len(bits) + n_coarse - 1):
-        sent = [0]
-        for b in bits[:k]:
-            sent = sent + [x + b for x in sent]
-        for x in sent:
-            dec_copy(flip(g, x, half), k).wait_send()
+        drain(dec.at[0, pl.ds(0, min(2 ** k, half))], dec_s.at[k])
 
 
 def local(
@@ -672,8 +601,7 @@
             pltpu.VMEM((heads * dec_rows, PAIR), bf16),
             pltpu.VMEM((heads * dec_rows, PAIR), f32),
             pltpu.VMEM((pairs, tokens, PAIR), bf16),
-            pltpu.VMEM((n_coarse, n_fine, tokens, PAIR), bf16),
-            pltpu.VMEM((n_coarse, n_fine, tokens, PAIR), bf16),
+            pltpu.VMEM((n_coarse, n_fine, 2, tokens, PAIR), bf16),
             pltpu.VMEM((pairs, 2 * tokens, PAIR), f32),
             pltpu.VMEM((pairs, 2 * tokens, PAIR), f32),
             pltpu.VMEM((pairs, tokens, PAIR), bf16),
@@ -686,20 +614,17 @@
             pltpu.VMEM((pairs // LOW, tokens, PAIR), bf16),
             pltpu.VMEM((pairs // LOW, tokens, PAIR), bf16),
             pltpu.VMEM((2, tokens, 3 * tokens), f32),
-            dma((8,)),
-            dma((2 * n_q - 1,)), dma((n_kv, n_q)),
-            dma((n_q,)), dma((LOW, n_coarse, n_q)),
-            dma((pairs,)), dma((pairs,)),
-            dma((n_fine,)), dma((n_coarse, n_fine)),
-            dma((n_fine,)), dma((n_coarse, n_fine)),
-            dma((n_fine, n_coarse)), dma((n_fine, n_coarse)),
+            dma((6,)),
+            dma, dma((2 * n_q + 1,)), dma, dma,
+            dma, dma((2,)),
+            dma, dma((n_fine + 2,)), dma,
             pltpu.SemaphoreType.REGULAR((n_q,)),
-            dma((3,)), dma((3,)),
-            dma((2, 2)), dma((2, 2)),
+            dma, dma((2,)),
+            dma((2,)), dma((2,)),
             dma, dma,
-            dma((pairs,)), dma((pairs,)),
-            dma((pairs // LOW,)), dma((pairs // LOW,)),
-            dma((n_bits + n_coarse - 1, half)), dma((n_coarse, half)),
+            dma, dma,
+            dma, dma,
+            dma((n_bits + n_coarse - 1,)), dma((half + 1,)),
         ],
         compiler_params=pltpu.CompilerParams(
             collective_id=0, has_side_effects=True, vmem_limit_bytes=32 * 1024 * 1024

time: 52.7 us -> 51.2 us (0.972)
  Pallas kernels: 50.2 us -> 48.7 us
    pallas_call x1, Pallas kernels: 50.2 us -> 48.7 us  [local(): pl.pallas_call(functools.partial(kernel, (n_coarse, n_fine, tokens, width...]
where the time goes in v4:
time: 51.2 us; the launch traced here: 51 us
  Pallas kernels  48.7 us (95%)
  local copies, waits for them, and re-layouts  1.67 us (3%)
  between operations  0.64 us (1%)
    pallas_call x1, Pallas kernels, local(): pl.pallas_call(functools.partial(kernel, (n_coarse, n_fine, tokens, width...  48.7 us
    unnamed x2, local copies, waits for them, and re-layouts  1.67 us

profile of v4, /device:TPU:0, one launch (start us, length us, event | category | flops | bytes accessed | tf_op | source)
XLA Modules:
  0.0 51.0 jit_solution(10245449773143523384)
XLA Ops:
  0.6 48.7 %shard_map.95 = (bf16[128,1024]{1,0:T(8,128)(2,1)S(1)}, bf16[2,4,64,1024]{3,2,1,0:T(8,128)(2,1)S(1)}) custom-call(bf16[128,1024]{1,0:T(8,128)(2,1)} %bitcast.13, bf16[128,1024]{1,0:T(8,128)(2,1)} %bitcast.14, bf16[128,1024]{1,0:T(8,128)(2,1)} %bitcast.15, bf16[128,1024]{1,0:T(8,128)(2,1)} %bitcast.16, bf16[128,1024]{1,0:T(8,128)(2,1)} %bitcast.17, ...), custom_call_target="tpu_custom_call" | custom-call | tf_op jit(solution)/shard_map/pallas_call | solution.py:590
  49.4 0.7 %copy.12 = bf16[1,128,1024]{2,1,0:T(8,128)(2,1)} copy(bf16[1,128,1024]{2,1,0:T(8,128)(2,1)S(1)} %bitcast.11) | data formatting | bytes 524288
  50.1 1.0 %copy.13 = bf16[1,512,1024]{2,1,0:T(8,128)(2,1)} copy(bf16[1,512,1024]{2,1,0:T(8,128)(2,1)S(1)} %bitcast.10) | data formatting | bytes 2097152

commit v5 on v4

--- a/solution.py
+++ b/solution.py
@@ -105,6 +105,17 @@
             body(d)
             return carry
         lax.fori_loop(start, stop, step, 0)
+
+    def loop_two(start, stop, work, save):
+        def step(i, carry):
+            d = start + 2 * i
+            first, second = work(d), work(d + 1)
+            save(d, first)
+            save(d + 1, second)
+            return carry
+        lax.fori_loop(0, (stop - start) // 2, step, 0)
+        if (stop - start) % 2:
+            save(stop - 1, work(stop - 1))
 
     def begin(copies):
         for copy in copies:
@@ -420,7 +431,11 @@
         peak = jnp.max(s, axis=1, keepdims=True)
         e = jnp.exp(s - peak)
         total = jnp.sum(e, axis=1, keepdims=True)
-        acc[j] = dot(e.astype(jnp.bfloat16), heavy_values(hh))
+        return j, dot(e.astype(jnp.bfloat16), heavy_values(hh)), peak, total
+
+    def heavy_keep(d, result):
+        j, o, peak, total = result
+        acc[j] = o
         stat[j] = jnp.where(lane_2 == 0, peak, total)
 
     def heavy_second(j):
@@ -436,25 +451,25 @@
     loads[3].wait()
     take(qbuf.at[pl.ds(0, pairs // 2 - 1)], q_r.at[0])
     kv_others(0)
-    loop(0, pairs // 2, heavy_first)
+    loop_two(0, pairs // 2, heavy_first, heavy_keep)
     for t in range(2, n_q):
         enc_side(t)
     n_chunk = d_total // d_chunk
+    n_chunk = d_total // d_chunk
     take(qbuf.at[pl.ds(0, pairs // 2)], q_r.at[1])
-    loop(pairs // 2, pairs, heavy_first)
+    loop_two(pairs // 2, pairs, heavy_first, heavy_keep)
     for d in far[0 * quarter:1 * quarter]:
         kv_forward(d)
     take(encbuf.at[pl.ds(0, LOW * (n_coarse - 1))], enc_r.at[2 * n_q])
-
+    pltpu.make_async_copy(lk.at[pl.ds(0, 2)], lk.at[pl.ds(0, 2)], load_s.at[4]).wait()
+    for side in range(2):
+        halo_send(side, lo == side)
     loop(0 * n_chunk // 4, 1 * n_chunk // 4, dec_step)
     for d in far[1 * quarter:2 * quarter]:
         kv_forward(d)
     loop(1 * n_chunk // 4, 2 * n_chunk // 4, dec_step)
     for d in far[2 * quarter:3 * quarter]:
         kv_forward(d)
-    pltpu.make_async_copy(lk.at[pl.ds(0, 2)], lk.at[pl.ds(0, 2)], load_s.at[4]).wait()
-    for side in range(2):
-        halo_send(side, lo == side)
     loop(2 * n_chunk // 4, 3 * n_chunk // 4, dec_step)
     for d in far[3 * quarter:4 * quarter]:
         kv_forward(d)
@@ -473,16 +488,20 @@
     dec_across(g)
     kv_others(1)
 
-    def heavy_out(i):
-        d = pairs - 1 - i
-        j = flip(p, d, pairs)
-        osend[j] = heavy_second(j)
-        o_copy(d).start()
-
-    loop(0, pairs // 2, heavy_out)
+    def heavy_end(i):
+        j = flip(p, pairs - 1 - i, pairs)
+        return j, heavy_second(j)
+
+    def heavy_out(i, result):
+        osend[result[0]] = result[1]
+        o_copy(pairs - 1 - i).start()
+
+    loop_two(0, pairs // 2, heavy_end, heavy_out)
     dec_wave(1)
-    loop(pairs // 2, pairs - 1, heavy_out)
-    orecv[p] = heavy_second(p)
+    loop_two(pairs // 2, pairs - 2, heavy_end, heavy_out)
+    near, home = heavy_end(pairs - 2), heavy_end(pairs - 1)
+    heavy_out(pairs - 2, near)
+    orecv[p] = home[1]
 
     take(lq.at[1 - lo], x_r.at[1])
     loads[7].wait()
@@ -507,17 +526,17 @@
         o = dot(e.astype(jnp.bfloat16), lv[pl.ds(b, 3), :, cols].reshape(3 * tokens, PAIR)) / total
         return jnp.where(low_half, o[:tokens], o[tokens:])
 
-    def light_away(j):
-        lsend[j] = light_of(1 - lo, j).astype(jnp.bfloat16)
+    def light_away(j, o):
+        lsend[j] = o.astype(jnp.bfloat16)
         light_back(j).start()
 
-    def light_home(j):
-        lown[:, cols_of(j)] = light_of(lo, j)
-
-    loop(0, pairs_half, light_away)
+    def light_home(j, o):
+        lown[:, cols_of(j)] = o
+
+    loop_two(0, pairs_half, lambda j: light_of(1 - lo, j), light_away)
     for steps in range(2, len(bits) + 1):
         dec_wave(steps)
-    loop(0, pairs_half, light_home)
+    loop_two(0, pairs_half, lambda j: light_of(lo, j), light_home)
 
     take(orecv.at[pl.ds(0, pairs - 1)], o_r)
 

time: 51.2 us -> 50.5 us (0.986)
  Pallas kernels: 48.7 us -> 47.7 us
    pallas_call x1, Pallas kernels: 48.7 us -> 47.7 us  [local(): pl.pallas_call(functools.partial(kernel, (n_coarse, n_fine, tokens, width...]
where the time goes in v5:
time: 50.5 us; the launch traced here: 50 us
  Pallas kernels  47.7 us (94%)
  local copies, waits for them, and re-layouts  1.67 us (3%)
  between operations  0.64 us (1%)
    pallas_call x1, Pallas kernels, local(): pl.pallas_call(functools.partial(kernel, (n_coarse, n_fine, tokens, width...  47.7 us
    unnamed x2, local copies, waits for them, and re-layouts  1.67 us

profile of v5, /device:TPU:0, one launch (start us, length us, event | category | flops | bytes accessed | tf_op | source)
XLA Modules:
  0.0 50.0 jit_solution(18424955002726279256)
XLA Ops:
  0.6 47.7 %shard_map.95 = (bf16[128,1024]{1,0:T(8,128)(2,1)S(1)}, bf16[2,4,64,1024]{3,2,1,0:T(8,128)(2,1)S(1)}) custom-call(bf16[128,1024]{1,0:T(8,128)(2,1)} %bitcast.13, bf16[128,1024]{1,0:T(8,128)(2,1)} %bitcast.14, bf16[128,1024]{1,0:T(8,128)(2,1)} %bitcast.15, bf16[128,1024]{1,0:T(8,128)(2,1)} %bitcast.16, bf16[128,1024]{1,0:T(8,128)(2,1)} %bitcast.17, ...), custom_call_target="tpu_custom_call" | custom-call | tf_op jit(solution)/shard_map/pallas_call | solution.py:609
  48.3 0.7 %copy.12 = bf16[1,128,1024]{2,1,0:T(8,128)(2,1)} copy(bf16[1,128,1024]{2,1,0:T(8,128)(2,1)S(1)} %bitcast.11) | data formatting | bytes 524288
  49.0 1.0 %copy.13 = bf16[1,512,1024]{2,1,0:T(8,128)(2,1)} copy(bf16[1,512,1024]{2,1,0:T(8,128)(2,1)S(1)} %bitcast.10) | data formatting | bytes 2097152

commit v6 on v5

--- a/solution.py
+++ b/solution.py
@@ -438,15 +438,24 @@
         acc[j] = o
         stat[j] = jnp.where(lane_2 == 0, peak, total)
 
-    def heavy_second(j):
-        s = heavy_scores(j, 1 - hh)
+    def heavy_more(d, cc):
+        j = flip(p, d, pairs)
+        part = 1 - hh
+        s = dot_t(stacked_pair(qbuf[j], low_half), kvbuf[cc, pl.ds(part * half, half), 0].reshape(half * tokens, PAIR))
+        if has_bias:
+            s = s + bias_ref[part, 0:1, pl.ds(pl.multiple_of(cc * half * tokens, PAIR), half * tokens)]
         before = stat[j, :, 0:1]
         peak = jnp.maximum(before, jnp.max(s, axis=1, keepdims=True))
         e = jnp.exp(s - peak)
         keep = jnp.exp(before - peak)
         total = stat[j, :, 1:2] * keep + jnp.sum(e, axis=1, keepdims=True)
-        o = (acc[j] * keep + dot(e.astype(jnp.bfloat16), heavy_values(1 - hh))) / total
-        return jnp.where(low_half, o[:tokens], o[tokens:]).astype(jnp.bfloat16)
+        values = kvbuf[cc, pl.ds(part * half, half), 1].reshape(half * tokens, PAIR)
+        return j, acc[j] * keep + dot(e.astype(jnp.bfloat16), values), peak, total
+
+    def heavy_last(d, cc):
+        j, o, peak, total = heavy_more(d, cc)
+        o = o / total
+        return j, jnp.where(low_half, o[:tokens], o[tokens:]).astype(jnp.bfloat16)
 
     loads[3].wait()
     take(qbuf.at[pl.ds(0, pairs // 2 - 1)], q_r.at[0])
@@ -484,13 +493,15 @@
     take(lk.at[pl.ds(0, 2)], x_r.at[0])
     for side in range(2):
         halo_send(side, lo == 1 - side)
+    dec_across(g)
+    loop_two(0, pairs, lambda d: heavy_more(d, c), heavy_keep)
     hop_forward()
-    dec_across(g)
     kv_others(1)
+    for e in range(1, n_coarse - 1):
+        loop_two(0, pairs, lambda d: heavy_more(d, up(c, e, n_coarse)), heavy_keep)
 
     def heavy_end(i):
-        j = flip(p, pairs - 1 - i, pairs)
-        return j, heavy_second(j)
+        return heavy_last(pairs - 1 - i, up(c, n_coarse - 1, n_coarse))
 
     def heavy_out(i, result):
         osend[result[0]] = result[1]

time: 50.5 us -> 50.5 us (level)
  the two profiles are of different devices: /device:TPU:0 before, /device:TPU:4 now
where the time goes in v6:
time: 50.5 us; the launch traced here: 50.4 us
  Pallas kernels  48.1 us (95%)
  local copies, waits for them, and re-layouts  1.67 us (3%)
  between operations  0.64 us (1%)
    pallas_call x1, Pallas kernels, local(): pl.pallas_call(functools.partial(kernel, (n_coarse, n_fine, tokens, width...  48.1 us
    unnamed x2, local copies, waits for them, and re-layouts  1.67 us

profile of v6, /device:TPU:4, one launch (start us, length us, event | category | flops | bytes accessed | tf_op | source)
XLA Modules:
  0.0 50.4 jit_solution(17697948106648207549)
XLA Ops:
  0.6 48.1 %shard_map.95 = (bf16[128,1024]{1,0:T(8,128)(2,1)S(1)}, bf16[2,4,64,1024]{3,2,1,0:T(8,128)(2,1)S(1)}) custom-call(bf16[128,1024]{1,0:T(8,128)(2,1)} %bitcast.13, bf16[128,1024]{1,0:T(8,128)(2,1)} %bitcast.14, bf16[128,1024]{1,0:T(8,128)(2,1)} %bitcast.15, bf16[128,1024]{1,0:T(8,128)(2,1)} %bitcast.16, bf16[128,1024]{1,0:T(8,128)(2,1)} %bitcast.17, ...), custom_call_target="tpu_custom_call" | custom-call | tf_op jit(solution)/shard_map/pallas_call | solution.py:620
  48.7 0.7 %copy.12 = bf16[1,128,1024]{2,1,0:T(8,128)(2,1)} copy(bf16[1,128,1024]{2,1,0:T(8,128)(2,1)S(1)} %bitcast.11) | data formatting | bytes 524288
  49.4 1.0 %copy.13 = bf16[1,512,1024]{2,1,0:T(8,128)(2,1)} copy(bf16[1,512,1024]{2,1,0:T(8,128)(2,1)S(1)} %bitcast.10) | data formatting | bytes 2097152
